TPU v7x, 32 devices: a whole 2x2x4 slice. The times are simulated.
32 devices in a mesh: outer: 8 (over z, core), inner: 4 (over y, x).
Axes of the slice: x: 2, y: 2, z: 4, core: 2. Of those that a mesh axis runs over, the one named last changes fastest.
Arguments:
- queries: bfloat16 [65536, 512], P(('outer', 'inner')), may hold values from -6 to 6
- inv_sqrt_degree: float32 [65536], P(('outer', 'inner')), may hold values from 0.35 to 1
- leaf_blocks: bfloat16 [512, 12, 128, 128], P(('outer', 'inner')), may hold values from -0.15625 to 0.15625
- block_cols: int32 [512, 12], P(('outer', 'inner')), may hold values from 0 to 15, as said below
- left_upper: bfloat16 [65536, 128], P(('outer', 'inner')), may hold values from -0.5 to 0.5
- right_upper: bfloat16 [65536, 128], P(('outer', 'inner')), may hold values from -0.03125 to 0.03125
- left_lower: bfloat16 [65536, 128], P(('outer', 'inner')), may hold values from -0.5 to 0.5
- right_lower: bfloat16 [65536, 128], P(('outer', 'inner')), may hold values from -0.09375 to 0.09375
Outputs:
- ranking: float32 [65536, 512], P(('outer', 'inner'))
Inputs may be any that keep to these rules, and one draw needn't show every extreme that they name: `block_cols`: in each block row the 12 block columns are distinct and count blocks from the first row of the same device's 2048 rows; the first of them is the row's own block.
All inputs are finite; a program needn't handle non-finite values.
Results may differ from a plain program's by a relative error of at most 0.0033.
Values sent between devices are 32-bit elements; how exact they have to be, the bound alone decides.
No kernel may reach another device: no remote copies, remote signals or barrier semaphores. Data moves between devices by JAX's collectives and lax.ppermute only.
A program may use at most 64 MiB of HBM per device.

v0:
```python
import jax
import jax.numpy as jnp
from jax import lax
from jax.sharding import PartitionSpec as P

ITERS = 2


damping = 0.9


def from_partner(value, axis, bit):
    mask = 2**bit
    pairs = [(source, source ^ mask) for source in range(lax.axis_size(axis))]
    return lax.ppermute(value, axis, pairs)


def project(basis, scaled):
    return lax.dot_general(
        basis, scaled, (((0,), (0,)), ((), ())), preferred_element_type=jnp.float32
    )


def lower_sums(upper_part, lower_part, inner_bits):
    for bit_number in range(inner_bits - 1):
        received = from_partner((upper_part, lower_part), "inner", bit_number)
        upper_part = upper_part + received[0]
        lower_part = lower_part + received[1]
    received = from_partner((upper_part, lower_part), "inner", inner_bits - 1)
    return (upper_part + received[0], damping * received[1])


def upper_sums(upper_part, outer_bits):
    for bit_number in range(outer_bits - 1):
        upper_part = upper_part + from_partner(upper_part, "outer", bit_number)
    return damping * from_partner(upper_part, "outer", outer_bits - 1)


def body(
    queries,
    inv_sqrt_degree,
    leaf_blocks,
    block_cols,
    left_upper,
    right_upper,
    left_lower,
    right_lower,
):
    inner_size = lax.axis_size("inner")
    outer_size = lax.axis_size("outer")
    inner_bits = inner_size.bit_length() - 1
    outer_bits = outer_size.bit_length() - 1
    row_count, query_count = queries.shape
    leaf_count = leaf_blocks.shape[0]
    col_table = (
        block_cols[:, :, None] == jnp.arange(leaf_count, dtype=jnp.int32)[None, None, :]
    ).astype(jnp.bfloat16)
    dense_leaf = jnp.einsum(
        "bjxy,bjc->bxcy", leaf_blocks, col_table, preferred_element_type=jnp.float32
    )
    dense_leaf = dense_leaf.astype(jnp.bfloat16).reshape(row_count, row_count)
    iterate = queries.astype(jnp.float32)
    for sweep in range(ITERS):
        scaled = (inv_sqrt_degree[:, None] * iterate).astype(jnp.bfloat16)
        upper_part = project(right_upper, scaled)
        lower_part = project(right_lower, scaled)
        upper_part, lower_sib = lower_sums(upper_part, lower_part, inner_bits)
        upper_sib = upper_sums(upper_part, outer_bits)
        leaf_term = jnp.dot(dense_leaf, scaled, preferred_element_type=jnp.float32)
        coupled = jnp.dot(
            left_upper, upper_sib.astype(jnp.bfloat16), preferred_element_type=jnp.float32
        )
        coupled = coupled + jnp.dot(
            left_lower, lower_sib.astype(jnp.bfloat16), preferred_element_type=jnp.float32
        )
        iterate = queries.astype(jnp.float32) + inv_sqrt_degree[:, None] * (
            damping * leaf_term + coupled
        )
    return iterate


def solution(mesh):
    return jax.shard_map(
        body,
        mesh=mesh,
        in_specs=(
            P(("outer", "inner"), None),
            P(("outer", "inner")),
            P(("outer", "inner"), None, None, None),
            P(("outer", "inner"), None),
            P(("outer", "inner"), None),
            P(("outer", "inner"), None),
            P(("outer", "inner"), None),
            P(("outer", "inner"), None),
        ),
        out_specs=P(("outer", "inner"), None),
        check_vma=False,
    )
```

profile of v0, /device:TPU:0, one launch (start us, length us, event | category | flops | bytes accessed | tf_op | source)
XLA Modules:
  0.0 96.2 jit_solution(516871575473458841)
XLA Ops:
  0.0 0.0 copy-start
  0.0 0.0 copy-start.6
  0.0 0.0 copy-start.2
  0.0 0.0 copy-start.5
  0.0 3.0 %convolution_bitcast_fusion.3 = f32[128,512]{0,1:T(8,128)S(1)} fusion(bf16[2048,128]{1,0:T(8,128)(2,1)} %param.13, bf16[2048,512]{1,0:T(8,128)(2,1)} %param.8, f32[2048]{0:T(1024)} %param.9), kind=kOutput, calls=%fused_computation.22 | convolution fusion | flops 271581184 | bytes 2891776 | tf_op jit(solution)/shard_map/dot_general | solution.py:19
  3.0 0.0 copy-start.1
  3.0 0.0 copy-start.7
  3.0 3.0 %collective-permute-start = (f32[128,512]{0,1:T(8,128)S(1)}, f32[128,512]{0,1:T(8,128)S(1)}, u32[]{:S(2)}, u32[]{:S(2)}) collective-permute-start(f32[128,512]{0,1:T(8,128)S(1)} %convolution_bitcast_fusion.3), channel_id=1, source_target_pairs={{0,1},{1,0},{2,3},{3,2},{4,5},{5,4},{6,7},{7,6},{8,9},{9,8},{10,11... | collective-permute-start | bytes 786440 | tf_op jit(solution)/shard_map/ppermute | solution.py:15
  6.0 6.3 %collective-permute-done = f32[128,512]{0,1:T(8,128)S(1)} collective-permute-done((f32[128,512]{0,1:T(8,128)S(1)}, f32[128,512]{0,1:T(8,128)S(1)}, u32[]{:S(2)}, u32[]{:S(2)}) %collective-permute-start) | collective-permute-done | bytes 262176 | tf_op jit(solution)/shard_map/ppermute | solution.py:15
  12.3 1.8 %collective-permute-start.1 = (f32[128,512]{0,1:T(8,128)S(1)}, f32[128,512]{0,1:T(8,128)S(1)}, u32[]{:S(2)}, u32[]{:S(2)}) collective-permute-start(f32[128,512]{0,1:T(8,128)S(1)} %add.54), channel_id=1, source_target_pairs={{0,2},{1,3},{2,0},{3,1},{4,6},{5,7},{6,4},{7,5},{8,10},{9,11},{10,... | collective-permute-start | bytes 786440 | tf_op jit(solution)/shard_map/ppermute | solution.py:15
  14.2 0.0 copy-done.6
  14.2 0.0 copy-done.2
  14.2 0.0 copy-done.5
  14.2 1.1 %convolution_bitcast_fusion.2 = f32[128,512]{0,1:T(8,128)S(1)} fusion(bf16[2048,128]{1,0:T(8,128)(2,1)S(1)} %copy-done.5, bf16[2048,512]{1,0:T(8,128)(2,1)S(1)} %copy-done.2, f32[2048]{0:T(1024)S(1)} %copy-done.6), kind=kOutput, calls=%fused_computation.21 | convolution fusion | flops 271581184 | bytes 2891776 | tf_op jit(solution)/shard_map/dot_general | solution.py:19
  15.3 1.6 %collective-permute-start.5 = (f32[128,512]{0,1:T(8,128)S(1)}, f32[128,512]{0,1:T(8,128)S(1)}, u32[]{:S(2)}, u32[]{:S(2)}) collective-permute-start(f32[128,512]{0,1:T(8,128)S(1)} %convolution_bitcast_fusion.2), channel_id=1, source_target_pairs={{0,1},{1,0},{2,3},{3,2},{4,5},{5,4},{6,7},{7,6},{8,9},{9,8},{10,11... | collective-permute-start | bytes 786440 | tf_op jit(solution)/shard_map/ppermute | solution.py:15
  16.9 3.0 %collective-permute-done.1 = f32[128,512]{0,1:T(8,128)S(1)} collective-permute-done((f32[128,512]{0,1:T(8,128)S(1)}, f32[128,512]{0,1:T(8,128)S(1)}, u32[]{:S(2)}, u32[]{:S(2)}) %collective-permute-start.1) | collective-permute-done | bytes 262176 | tf_op jit(solution)/shard_map/ppermute | solution.py:15
  19.9 0.1 collective-permute-start.2
  20.0 0.0 copy-done.1
  20.0 0.0 copy-done.7
  20.0 7.1 %fusion.8 = bf16[16,16,128,128]{3,1,2,0:T(8,128)(2,1)} fusion(bf16[16,12,128,128]{3,2,1,0:T(8,128)(2,1)S(1)} %copy-done.1, s32[16,12]{1,0:T(8,128)S(1)} %copy-done.7), kind=kOutput, calls=%fused_computation.8 | convolution fusion | flops 104860672 | bytes 14680832 | tf_op jit(solution)/shard_map/bjxy,bjc->bxcy/dot_general | solution.py:58
  27.2 0.0 collective-permute-done.5
  27.2 1.5 %collective-permute-start.6 = (f32[128,512]{0,1:T(8,128)S(1)}, f32[128,512]{0,1:T(8,128)S(1)}, u32[]{:S(2)}, u32[]{:S(2)}) collective-permute-start(f32[128,512]{0,1:T(8,128)S(1)} %add.58), channel_id=1, source_target_pairs={{0,2},{1,3},{2,0},{3,1},{4,6},{5,7},{6,4},{7,5},{8,10},{9,11},{10,... | collective-permute-start | bytes 786440 | tf_op jit(solution)/shard_map/ppermute | solution.py:15
  28.7 0.0 collective-permute-done.2
  28.8 1.6 %collective-permute-start.3 = (f32[128,512]{0,1:T(8,128)S(1)}, f32[128,512]{0,1:T(8,128)S(1)}, u32[]{:S(2)}, u32[]{:S(2)}) collective-permute-start(f32[128,512]{0,1:T(8,128)S(1)} %add.56), channel_id=1, source_target_pairs={{0,8},{4,12},{8,0},{12,4},{16,24},{20,28},{24,16},{28,20},{1,9},{5... | collective-permute-start | bytes 786440 | tf_op jit(solution)/shard_map/ppermute | solution.py:15
  30.4 7.0 %fusion.2 = f32[2048,512]{1,0:T(8,128)S(1)} fusion(bf16[256,8,16,128]{3,2,1,0:T(8,128)(2,1)} %bitcast.44, bf16[2048,512]{1,0:T(8,128)(2,1)S(1)} %copy-done.2, f32[2048]{0:T(1024)S(1)} %copy-done.6), kind=kOutput, calls=%fused_computation.2 | convolution fusion | flops 4298113024 | bytes 14688256 | tf_op jit(solution)/shard_map/dot_general | solution.py:69
  37.4 0.0 copy-start.3
  37.4 0.0 collective-permute-done.3
  37.5 2.7 %collective-permute-start.4 = (f32[128,512]{0,1:T(8,128)S(1)}, f32[128,512]{0,1:T(8,128)S(1)}, u32[]{:S(2)}, u32[]{:S(2)}) collective-permute-start(f32[128,512]{0,1:T(8,128)S(1)} %add.57), channel_id=1, source_target_pairs={{0,16},{4,20},{8,24},{12,28},{16,0},{20,4},{24,8},{28,12},{1,17},{... | collective-permute-start | bytes 786440 | tf_op jit(solution)/shard_map/ppermute | solution.py:15
  40.2 0.0 collective-permute-done.6
  40.2 0.0 copy-done
  40.2 0.0 slice-start
  40.2 0.7 fusion.16
  40.9 0.0 copy-start.4
  40.9 0.0 slice-start.1
  40.9 11.3 %collective-permute-done.4 = f32[128,512]{0,1:T(8,128)S(1)} collective-permute-done((f32[128,512]{0,1:T(8,128)S(1)}, f32[128,512]{0,1:T(8,128)S(1)}, u32[]{:S(2)}, u32[]{:S(2)}) %collective-permute-start.4) | collective-permute-done | bytes 262176 | tf_op jit(solution)/shard_map/ppermute | solution.py:15
  52.2 0.0 copy-done.3
  52.2 1.7 %fusion.13 = bf16[2048,512]{1,0:T(8,128)(2,1)S(1)} fusion(bf16[2048,512]{1,0:T(8,128)(2,1)S(1)} %copy-done.2, f32[512,2048]{0,1:T(8,128)S(1)} %fusion.16, f32[2048,512]{1,0:T(8,128)S(1)} %fusion.2, bf16[2048,128]{1,0:T(8,128)(2,1)S(1)} %copy-done.3, f32[2048]{0:T(1024)S(1)} %copy-done.6, f32[128,512]{0,1:T(8,128)S(1)} %collective-permute-done.4), kind=kOutput, calls=%fused_computation.14 | convolution fusion | flops 276955136 | bytes 13377536 | tf_op jit(solution)/shard_map/dot_general | solution.py:70
  53.9 0.0 copy-done.4
  53.9 0.7 convolution_bitcast_fusion.1
  54.6 1.5 %collective-permute-start.7 = (f32[128,512]{0,1:T(8,128)S(1)}, f32[128,512]{0,1:T(8,128)S(1)}, u32[]{:S(2)}, u32[]{:S(2)}) collective-permute-start(f32[128,512]{0,1:T(8,128)S(1)} %convolution_bitcast_fusion.1), channel_id=1, source_target_pairs={{0,1},{1,0},{2,3},{3,2},{4,5},{5,4},{6,7},{7,6},{8,9},{9,8},{10,11... | collective-permute-start | bytes 786440 | tf_op jit(solution)/shard_map/ppermute | solution.py:15
  56.2 6.5 %collective-permute-done.7 = f32[128,512]{0,1:T(8,128)S(1)} collective-permute-done((f32[128,512]{0,1:T(8,128)S(1)}, f32[128,512]{0,1:T(8,128)S(1)}, u32[]{:S(2)}, u32[]{:S(2)}) %collective-permute-start.7) | collective-permute-done | bytes 262176 | tf_op jit(solution)/shard_map/ppermute | solution.py:15
  62.7 0.6 collective-permute-start.8
  63.3 0.7 convolution_bitcast_fusion
  64.1 1.6 %collective-permute-start.12 = (f32[128,512]{0,1:T(8,128)S(1)}, f32[128,512]{0,1:T(8,128)S(1)}, u32[]{:S(2)}, u32[]{:S(2)}) collective-permute-start(f32[128,512]{0,1:T(8,128)S(1)} %convolution_bitcast_fusion), channel_id=1, source_target_pairs={{0,1},{1,0},{2,3},{3,2},{4,5},{5,4},{6,7},{7,6},{8,9},{9,8},{10,11... | collective-permute-start | bytes 786440 | tf_op jit(solution)/shard_map/ppermute | solution.py:15
  65.6 4.3 %collective-permute-done.8 = f32[128,512]{0,1:T(8,128)S(1)} collective-permute-done((f32[128,512]{0,1:T(8,128)S(1)}, f32[128,512]{0,1:T(8,128)S(1)}, u32[]{:S(2)}, u32[]{:S(2)}) %collective-permute-start.8) | collective-permute-done | bytes 262176 | tf_op jit(solution)/shard_map/ppermute | solution.py:15
  70.0 0.1 collective-permute-start.9
  70.0 0.9 collective-permute-done.12
  71.0 1.6 %collective-permute-start.13 = (f32[128,512]{0,1:T(8,128)S(1)}, f32[128,512]{0,1:T(8,128)S(1)}, u32[]{:S(2)}, u32[]{:S(2)}) collective-permute-start(f32[128,512]{0,1:T(8,128)S(1)} %add.67), channel_id=1, source_target_pairs={{0,2},{1,3},{2,0},{3,1},{4,6},{5,7},{6,4},{7,5},{8,10},{9,11},{10,... | collective-permute-start | bytes 786440 | tf_op jit(solution)/shard_map/ppermute | solution.py:15
  72.6 0.0 collective-permute-done.9
  72.6 0.1 collective-permute-start.10
  72.7 0.0 slice-done
  72.7 0.0 slice-done.1
  72.7 4.5 %fusion = f32[2048,512]{1,0:T(8,128)S(1)} fusion(bf16[2048,512]{1,0:T(8,128)(2,1)S(1)} %fusion.13, bf16[256,8,16,128]{3,2,1,0:T(8,128)(2,1)S(1)} %bitcast.47), kind=kOutput, calls=%fused_computation | convolution fusion | flops 4294967296 | bytes 14680064 | tf_op jit(solution)/shard_map/dot_general | solution.py:69
  77.3 2.7 %collective-permute-done.10 = f32[128,512]{0,1:T(8,128)S(1)} collective-permute-done((f32[128,512]{0,1:T(8,128)S(1)}, f32[128,512]{0,1:T(8,128)S(1)}, u32[]{:S(2)}, u32[]{:S(2)}) %collective-permute-start.10) | collective-permute-done | bytes 262176 | tf_op jit(solution)/shard_map/ppermute | solution.py:15
  80.0 0.6 collective-permute-start.11
  80.7 0.0 collective-permute-done.13
  80.7 0.7 fusion.17
  81.4 11.6 %collective-permute-done.11 = f32[128,512]{0,1:T(8,128)S(1)} collective-permute-done((f32[128,512]{0,1:T(8,128)S(1)}, f32[128,512]{0,1:T(8,128)S(1)}, u32[]{:S(2)}, u32[]{:S(2)}) %collective-permute-start.11) | collective-permute-done | bytes 262176 | tf_op jit(solution)/shard_map/ppermute | solution.py:15
  93.0 3.2 %convert_add_fusion = f32[2048,512]{1,0:T(8,128)} fusion(bf16[2048,512]{1,0:T(8,128)(2,1)S(1)} %copy-done.2, f32[512,2048]{0,1:T(8,128)S(1)} %fusion.17, f32[2048,512]{1,0:T(8,128)S(1)} %fusion, bf16[2048,128]{1,0:T(8,128)(2,1)S(1)} %copy-done.3, f32[2048]{0:T(1024)S(1)} %copy-done.6, f32[128,512]{0,1:T(8,128)S(1)} %collective-permute-done.11), kind=kOutput, calls=%fused_computation.9 | convolution fusion | flops 274857984 | bytes 15474688 | tf_op jit(solution)/shard_map/dot_general | solution.py:70
  (11 shorter events, 0.3 us)
Async XLA Ops:
  0.0 40.2 %copy-start = (bf16[2048,128]{1,0:T(8,128)(2,1)S(1)}, bf16[2048,128]{1,0:T(8,128)(2,1)}, u32[]{:S(2)}) copy-start(bf16[2048,128]{1,0:T(8,128)(2,1)} %param.14) | copy-start | bytes 1572868
  0.0 14.2 %copy-start.6 = (f32[2048]{0:T(1024)S(1)}, f32[2048]{0:T(1024)}, u32[]{:S(2)}) copy-start(f32[2048]{0:T(1024)} %param.9) | copy-start | bytes 24580
  0.0 14.2 %copy-start.2 = (bf16[2048,512]{1,0:T(8,128)(2,1)S(1)}, bf16[2048,512]{1,0:T(8,128)(2,1)}, u32[]{:S(2)}) copy-start(bf16[2048,512]{1,0:T(8,128)(2,1)} %param.8) | copy-start | bytes 6291460
  0.0 14.2 %copy-start.5 = (bf16[2048,128]{1,0:T(8,128)(2,1)S(1)}, bf16[2048,128]{1,0:T(8,128)(2,1)}, u32[]{:S(2)}) copy-start(bf16[2048,128]{1,0:T(8,128)(2,1)} %param.15) | copy-start | bytes 1572868
  3.0 17.0 %copy-start.1 = (bf16[16,12,128,128]{3,2,1,0:T(8,128)(2,1)S(1)}, bf16[16,12,128,128]{3,2,1,0:T(8,128)(2,1)}, u32[]{:S(2)}) copy-start(bf16[16,12,128,128]{3,2,1,0:T(8,128)(2,1)} %param.10) | copy-start | bytes 18874372
  3.0 17.0 %copy-start.7 = (s32[16,12]{1,0:T(8,128)S(1)}, s32[16,12]{1,0:T(8,128)}, u32[]{:S(2)}) copy-start(s32[16,12]{1,0:T(8,128)} %param.11) | copy-start | bytes 2308
  3.0 9.3 %collective-permute-start = (f32[128,512]{0,1:T(8,128)S(1)}, f32[128,512]{0,1:T(8,128)S(1)}, u32[]{:S(2)}, u32[]{:S(2)}) collective-permute-start(f32[128,512]{0,1:T(8,128)S(1)} %convolution_bitcast_fusion.3), channel_id=1, source_target_pairs={{0,1},{1,0},{2,3},{3,2},{4,5},{5,4},{6,7},{7,6},{8,9},{9,8},{10,11... | collective-permute-start | bytes 786440 | tf_op jit(solution)/shard_map/ppermute | solution.py:15
  12.3 7.6 %collective-permute-start.1 = (f32[128,512]{0,1:T(8,128)S(1)}, f32[128,512]{0,1:T(8,128)S(1)}, u32[]{:S(2)}, u32[]{:S(2)}) collective-permute-start(f32[128,512]{0,1:T(8,128)S(1)} %add.54), channel_id=1, source_target_pairs={{0,2},{1,3},{2,0},{3,1},{4,6},{5,7},{6,4},{7,5},{8,10},{9,11},{10,... | collective-permute-start | bytes 786440 | tf_op jit(solution)/shard_map/ppermute | solution.py:15
  15.3 11.8 %collective-permute-start.5 = (f32[128,512]{0,1:T(8,128)S(1)}, f32[128,512]{0,1:T(8,128)S(1)}, u32[]{:S(2)}, u32[]{:S(2)}) collective-permute-start(f32[128,512]{0,1:T(8,128)S(1)} %convolution_bitcast_fusion.2), channel_id=1, source_target_pairs={{0,1},{1,0},{2,3},{3,2},{4,5},{5,4},{6,7},{7,6},{8,9},{9,8},{10,11... | collective-permute-start | bytes 786440 | tf_op jit(solution)/shard_map/ppermute | solution.py:15
  19.9 8.8 %collective-permute-start.2 = (f32[128,512]{0,1:T(8,128)S(1)}, f32[128,512]{0,1:T(8,128)S(1)}, u32[]{:S(2)}, u32[]{:S(2)}) collective-permute-start(f32[128,512]{0,1:T(8,128)S(1)} %add.55), channel_id=1, source_target_pairs={{0,4},{4,0},{8,12},{12,8},{16,20},{20,16},{24,28},{28,24},{1,5},{5... | collective-permute-start | bytes 786440 | tf_op jit(solution)/shard_map/ppermute | solution.py:15
  27.2 13.0 %collective-permute-start.6 = (f32[128,512]{0,1:T(8,128)S(1)}, f32[128,512]{0,1:T(8,128)S(1)}, u32[]{:S(2)}, u32[]{:S(2)}) collective-permute-start(f32[128,512]{0,1:T(8,128)S(1)} %add.58), channel_id=1, source_target_pairs={{0,2},{1,3},{2,0},{3,1},{4,6},{5,7},{6,4},{7,5},{8,10},{9,11},{10,... | collective-permute-start | bytes 786440 | tf_op jit(solution)/shard_map/ppermute | solution.py:15
  28.8 8.7 %collective-permute-start.3 = (f32[128,512]{0,1:T(8,128)S(1)}, f32[128,512]{0,1:T(8,128)S(1)}, u32[]{:S(2)}, u32[]{:S(2)}) collective-permute-start(f32[128,512]{0,1:T(8,128)S(1)} %add.56), channel_id=1, source_target_pairs={{0,8},{4,12},{8,0},{12,4},{16,24},{20,28},{24,16},{28,20},{1,9},{5... | collective-permute-start | bytes 786440 | tf_op jit(solution)/shard_map/ppermute | solution.py:15
  37.4 14.8 %copy-start.3 = (bf16[2048,128]{1,0:T(8,128)(2,1)S(1)}, bf16[2048,128]{1,0:T(8,128)(2,1)}, u32[]{:S(2)}) copy-start(bf16[2048,128]{1,0:T(8,128)(2,1)} %param.12) | copy-start | bytes 1572868
  37.5 14.7 %collective-permute-start.4 = (f32[128,512]{0,1:T(8,128)S(1)}, f32[128,512]{0,1:T(8,128)S(1)}, u32[]{:S(2)}, u32[]{:S(2)}) collective-permute-start(f32[128,512]{0,1:T(8,128)S(1)} %add.57), channel_id=1, source_target_pairs={{0,16},{4,20},{8,24},{12,28},{16,0},{20,4},{24,8},{28,12},{1,17},{... | collective-permute-start | bytes 786440 | tf_op jit(solution)/shard_map/ppermute | solution.py:15
  40.2 32.5 %slice-start = ((s8[8388608]{0:T(1024)(128)(4,1)}), s8[4194304]{0:T(1024)(128)(4,1)S(1)}, s32[]{:S(2)}) async-start(s8[8388608]{0:T(1024)(128)(4,1)} %bitcast.45), calls=%async_computation | async-start | bytes 8388608
  40.9 13.0 %copy-start.4 = (bf16[2048,128]{1,0:T(8,128)(2,1)S(1)}, bf16[2048,128]{1,0:T(8,128)(2,1)}, u32[]{:S(2)}) copy-start(bf16[2048,128]{1,0:T(8,128)(2,1)} %param.13) | copy-start | bytes 1572868
  40.9 31.8 %slice-start.1 = ((s8[8388608]{0:T(1024)(128)(4,1)}), s8[4194304]{0:T(1024)(128)(4,1)S(1)}, s32[]{:S(2)}) async-start(s8[8388608]{0:T(1024)(128)(4,1)} %bitcast.45), calls=%async_computation.1 | async-start | bytes 8388608
  54.6 8.1 %collective-permute-start.7 = (f32[128,512]{0,1:T(8,128)S(1)}, f32[128,512]{0,1:T(8,128)S(1)}, u32[]{:S(2)}, u32[]{:S(2)}) collective-permute-start(f32[128,512]{0,1:T(8,128)S(1)} %convolution_bitcast_fusion.1), channel_id=1, source_target_pairs={{0,1},{1,0},{2,3},{3,2},{4,5},{5,4},{6,7},{7,6},{8,9},{9,8},{10,11... | collective-permute-start | bytes 786440 | tf_op jit(solution)/shard_map/ppermute | solution.py:15
  62.7 7.2 %collective-permute-start.8 = (f32[128,512]{0,1:T(8,128)S(1)}, f32[128,512]{0,1:T(8,128)S(1)}, u32[]{:S(2)}, u32[]{:S(2)}) collective-permute-start(f32[128,512]{0,1:T(8,128)S(1)} %add.63), channel_id=1, source_target_pairs={{0,2},{1,3},{2,0},{3,1},{4,6},{5,7},{6,4},{7,5},{8,10},{9,11},{10,... | collective-permute-start | bytes 786440 | tf_op jit(solution)/shard_map/ppermute | solution.py:15
  64.1 6.9 %collective-permute-start.12 = (f32[128,512]{0,1:T(8,128)S(1)}, f32[128,512]{0,1:T(8,128)S(1)}, u32[]{:S(2)}, u32[]{:S(2)}) collective-permute-start(f32[128,512]{0,1:T(8,128)S(1)} %convolution_bitcast_fusion), channel_id=1, source_target_pairs={{0,1},{1,0},{2,3},{3,2},{4,5},{5,4},{6,7},{7,6},{8,9},{9,8},{10,11... | collective-permute-start | bytes 786440 | tf_op jit(solution)/shard_map/ppermute | solution.py:15
  70.0 2.6 %collective-permute-start.9 = (f32[128,512]{0,1:T(8,128)S(1)}, f32[128,512]{0,1:T(8,128)S(1)}, u32[]{:S(2)}, u32[]{:S(2)}) collective-permute-start(f32[128,512]{0,1:T(8,128)S(1)} %add.64), channel_id=1, source_target_pairs={{0,4},{4,0},{8,12},{12,8},{16,20},{20,16},{24,28},{28,24},{1,5},{5... | collective-permute-start | bytes 786440 | tf_op jit(solution)/shard_map/ppermute | solution.py:15
  71.0 9.7 %collective-permute-start.13 = (f32[128,512]{0,1:T(8,128)S(1)}, f32[128,512]{0,1:T(8,128)S(1)}, u32[]{:S(2)}, u32[]{:S(2)}) collective-permute-start(f32[128,512]{0,1:T(8,128)S(1)} %add.67), channel_id=1, source_target_pairs={{0,2},{1,3},{2,0},{3,1},{4,6},{5,7},{6,4},{7,5},{8,10},{9,11},{10,... | collective-permute-start | bytes 786440 | tf_op jit(solution)/shard_map/ppermute | solution.py:15
  72.6 7.4 %collective-permute-start.10 = (f32[128,512]{0,1:T(8,128)S(1)}, f32[128,512]{0,1:T(8,128)S(1)}, u32[]{:S(2)}, u32[]{:S(2)}) collective-permute-start(f32[128,512]{0,1:T(8,128)S(1)} %add.65), channel_id=1, source_target_pairs={{0,8},{4,12},{8,0},{12,4},{16,24},{20,28},{24,16},{28,20},{1,9},{5... | collective-permute-start | bytes 786440 | tf_op jit(solution)/shard_map/ppermute | solution.py:15
  80.0 13.0 %collective-permute-start.11 = (f32[128,512]{0,1:T(8,128)S(1)}, f32[128,512]{0,1:T(8,128)S(1)}, u32[]{:S(2)}, u32[]{:S(2)}) collective-permute-start(f32[128,512]{0,1:T(8,128)S(1)} %add.66), channel_id=1, source_target_pairs={{0,16},{4,20},{8,24},{12,28},{16,0},{20,4},{24,8},{28,12},{1,17},{... | collective-permute-start | bytes 786440 | tf_op jit(solution)/shard_map/ppermute | solution.py:15
where the time goes:
time: 96.4 us; the launch traced here: 96.2 us
  waiting for transfers between devices  46.8 us (49%)
  matrix products  30.6 us (32%)
  starting transfers between devices  18.3 us (19%)
    ppermute x14, waiting for transfers between devices, from_partner(): return lax.ppermute(value, axis, pairs)  46.8 us
    ppermute x14, starting transfers between devices, from_partner(): return lax.ppermute(value, axis, pairs)  18.3 us
    dot_general x2, matrix products, body(): leaf_term = jnp.dot(dense_leaf, scaled, preferred_element_type=jnp.float32)  11.6 us
    dot_general x1, matrix products, body(): jnp.einsum('bjxy,bjc->bxcy', leaf_blocks, col_table, preferred_element_ty...  7.14 us
    dot_general x4, matrix products, project(): lax.dot_general(basis, scaled, (((0,), (0,)), ((), ())), preferred_elemen...  5.58 us
    dot_general x2, matrix products, body(): jnp.dot(left_upper, upper_sib.astype(jnp.bfloat16), preferred_element_typ...  4.91 us
  transfers between devices with their start and end apart: 14, of which 8 were waited for; matrix products, arithmetic and copies ran while one was open for 23% of the time, Pallas kernels for 0%

commit v1 on v0

v1 whole, which is shorter than its diff:
```python
import jax
import jax.numpy as jnp
from jax import lax
from jax.experimental import pallas as pl
from jax.experimental.pallas import tpu as pltpu
from jax.sharding import Mesh
from jax.sharding import PartitionSpec as P

DAMPING = 0.9
F32 = jnp.float32
BF16 = jnp.bfloat16
VMEM = pl.BlockSpec(memory_space=pltpu.VMEM)
SMEM = pl.BlockSpec(memory_space=pltpu.SMEM)
FAR = pl.BlockSpec(memory_space=pltpu.HBM)


def shape(dims, dtype, near=False):
    return (pltpu.VMEM if near else pltpu.HBM)(dims, dtype)


def call(kernel, args, outs, scratch, megabytes, flops):
    values = [
        value if spec is SMEM else pltpu.with_memory_space_constraint(value, spec.memory_space)
        for value, spec in args
    ]
    return pl.pallas_call(
        kernel,
        out_shape=[out for out in outs],
        in_specs=[spec for _, spec in args],
        out_specs=[
            FAR if out.memory_space == pltpu.HBM else VMEM for out in outs
        ],
        scratch_shapes=scratch,
        cost_estimate=pl.CostEstimate(
            flops=flops, bytes_accessed=2**20, transcendentals=0
        ),
        compiler_params=pltpu.CompilerParams(vmem_limit_bytes=megabytes * 2**20),
    )(*values)


def dot(a, b):
    return jnp.dot(a, b, preferred_element_type=F32)


def tdot(a, b):
    return lax.dot_general(a, b, (((0,), (0,)), ((), ())), preferred_element_type=F32)


def start(source, target, sem):
    copy = pltpu.make_async_copy(source, target, sem)
    copy.start()
    return copy


def degree_columns(degree_ref):
    leaves, block = degree_ref.shape
    tall = jnp.concatenate([degree_ref[...]] * (block // leaves), axis=0)
    return tall.T[:, :leaves]


def scale_tile(columns, first, value):
    block = columns.shape[0]
    return jnp.concatenate(
        [
            columns[:, first + b : first + b + 1] * value[b * block : (b + 1) * block]
            for b in range(value.shape[0] // block)
        ],
        axis=0,
    )


def coupling_kernel(
    degree_hbm, lu_hbm, ll_hbm, ru_hbm, rl_hbm,
    spread_hbm, right_hbm, late_hbm, early_ref,
    degree_ref, lu_ref, ll_ref, ru_ref, rl_ref, spread_ref, right_ref, late_ref, sems,
):
    pairs = (
        (degree_hbm, degree_ref), (ll_hbm, ll_ref), (ru_hbm, ru_ref), (lu_hbm, lu_ref), (rl_hbm, rl_ref),
    )
    copies = [start(a, b, sems.at[i]) for i, (a, b) in enumerate(pairs)]
    leaves, block = degree_ref.shape
    rank = lu_ref.shape[1]
    copies[0].wait()
    columns = degree_columns(degree_ref)
    square = columns * columns

    def scaled(source, target, lanes):
        for leaf in range(leaves):
            rows = slice(leaf * block, (leaf + 1) * block)
            target[rows, lanes] = (
                square[:, leaf : leaf + 1] * source[rows, :].astype(F32)
            ).astype(BF16)

    copies[1].wait()
    scaled(ll_ref, spread_ref, slice(rank, 2 * rank))
    copies[2].wait()
    early_ref[...] = tdot(spread_ref[:, rank:], ru_ref[...])
    scaled(ru_ref, right_ref, slice(0, rank))
    copies[3].wait()
    scaled(lu_ref, spread_ref, slice(0, rank))
    out0 = start(spread_ref, spread_hbm, sems.at[5])
    late_ref[:rank, :] = tdot(spread_ref[:, :rank], ru_ref[...])
    copies[4].wait()
    scaled(rl_ref, right_ref, slice(rank, 2 * rank))
    out1 = start(right_ref, right_hbm, sems.at[6])
    late_ref[rank:, :] = tdot(spread_ref[...], rl_ref[...])
    out2 = start(late_ref, late_hbm, sems.at[7])
    for out in (out0, out1, out2):
        out.wait()


def first_kernel(
    degree_hbm, y_hbm, ru_hbm, rl_hbm,
    scaled_hbm, coef_hbm, lower_ref,
    degree_ref, y_ref, right_ref, scaled_ref, coef_ref, sems,
):
    leaves, block = degree_ref.shape
    rank = ru_hbm.shape[1]
    tiles = 4
    size = y_ref.shape[0] // tiles
    copies = [start(degree_hbm, degree_ref, sems.at[0])]
    for tile in range(tiles):
        rows = pl.ds(tile * size, size)
        copies.append(start(y_hbm.at[rows], y_ref.at[rows], sems.at[1 + tile]))
    sides = [
        start(ru_hbm, right_ref.at[:, pl.ds(0, rank)], sems.at[9]),
        start(rl_hbm, right_ref.at[:, pl.ds(rank, rank)], sems.at[10]),
    ]
    copies[0].wait()
    columns = degree_columns(degree_ref)
    outs = []
    for tile in range(tiles):
        copies[1 + tile].wait()
        rows = slice(tile * size, (tile + 1) * size)
        value = y_ref[rows, :].astype(F32)
        scaled_ref[rows, :] = scale_tile(columns, tile * size // block, value).astype(BF16)
        near = pl.ds(tile * size, size)
        outs.append(start(scaled_ref.at[near], scaled_hbm.at[near], sems.at[5 + tile]))
    for copy in sides:
        copy.wait()
    coef_ref[...] = tdot(scaled_ref[...], right_ref[...])
    outs.append(start(coef_ref, coef_hbm, sems.at[0]))
    lower_ref[...] = coef_ref[:, rank:]
    for out in outs:
        out.wait()


def dense_kernel(
    cols_ref, blocks_hbm, scaled_hbm, right_hbm, coef_hbm, late_hbm, cross_ref,
    dense_hbm, low_hbm, both_ref,
    blocks_ref, dense_ref, scaled_ref, right_ref, coef_ref, late_ref, low_ref, sems,
):
    leaves, stored, block, _ = blocks_ref.shape
    copies = [
        start(blocks_hbm.at[row], blocks_ref.at[row], sems.at[row])
        for row in range(leaves)
    ]
    sides = [
        start(a, b, sems.at[leaves + i])
        for i, (a, b) in enumerate(
            ((right_hbm, right_ref), (scaled_hbm, scaled_ref), (coef_hbm, coef_ref), (late_hbm, late_ref))
        )
    ]
    outs = []
    for row in range(leaves):
        rows = slice(row * block, (row + 1) * block)
        dense_ref[rows, :] = jnp.zeros((block, leaves * block), BF16)
        copies[row].wait()
        for j in range(stored):
            col = pl.multiple_of(cols_ref[row, j] * block, block)
            dense_ref[rows, pl.ds(col, block)] = blocks_ref[row, j]
        near = pl.ds(row * block, block)
        outs.append(start(dense_ref.at[near], dense_hbm.at[near], sems.at[row]))
    for side in sides:
        side.wait()
    rank = cross_ref.shape[0]
    parts, height, _ = both_ref.shape
    through = tdot(right_ref[...], dense_ref[...]).astype(BF16)
    found = coef_ref[...] + DAMPING * dot(through, scaled_ref[...]).T
    second = found[:, :rank] + dot(
        coef_ref[:, rank:].astype(BF16), (DAMPING * cross_ref[...]).astype(BF16)
    )
    low_ref[: found.shape[0], :] = found[:, rank:]
    low_ref[found.shape[0] :, :] = late_ref[rank:, :]
    outs.append(start(low_ref, low_hbm, sems.at[leaves]))
    width = found.shape[0] // parts
    lines = rank // parts
    both_ref[:, :width, :] = coef_ref[:, :rank].reshape(parts, width, rank)
    both_ref[:, width : 2 * width, :] = second.reshape(parts, width, rank)
    for part in range(parts):
        both_ref[part, 2 * width : 2 * width + lines, :] = late_ref[
            part * lines : (part + 1) * lines, :
        ]
    for out in outs:
        out.wait()


def load_tiles(hbm, ref, tiles, sems, first):
    size = ref.shape[0] // tiles
    return [
        start(hbm.at[pl.ds(t * size, size)], ref.at[pl.ds(t * size, size)], sems.at[first + t])
        for t in range(tiles)
    ]


def known_kernel(
    degree_hbm, dense_hbm, scaled_hbm, spread_hbm, y_hbm,
    known_hbm, far_hbm,
    degree_ref, dense_ref, scaled_ref, spread_ref, y_ref, known_ref, far_ref, sems,
):
    tiles = 8
    block = degree_ref.shape[1]
    size = dense_ref.shape[0] // tiles
    sides = [
        start(a, b, sems.at[tiles + i])
        for i, (a, b) in enumerate(
            ((degree_hbm, degree_ref), (scaled_hbm, scaled_ref), (spread_hbm, spread_ref), (y_hbm, y_ref))
        )
    ]
    copies = load_tiles(dense_hbm, dense_ref, tiles, sems, 0)
    for side in sides:
        side.wait()
    columns = degree_columns(degree_ref)
    outs = []
    for tile in range(tiles):
        rows = slice(tile * size, (tile + 1) * size)
        near = pl.ds(tile * size, size)
        copies[tile].wait()
        product = dot(dense_ref[rows, :], scaled_ref[...])
        first = tile * size // block
        value = y_ref[rows, :].astype(F32) + DAMPING * scale_tile(columns, first, product)
        known_ref[rows, :] = scale_tile(columns, first, value).astype(BF16)
        far_ref[rows, :] = (DAMPING * dot(dense_ref[rows, :], spread_ref[...])).astype(BF16)
        outs.append(start(known_ref.at[near], known_hbm.at[near], sems.at[tile]))
        outs.append(start(far_ref.at[near], far_hbm.at[near], sems.at[tiles + tile]))
    for out in outs:
        out.wait()


def base_kernel(
    degree_hbm, dense_hbm, known_hbm, y_hbm,
    base_hbm,
    degree_ref, dense_ref, known_ref, y_ref, base_ref, sems,
):
    tiles = 8
    block = degree_ref.shape[1]
    size = dense_ref.shape[0] // tiles
    sides = [
        start(a, b, sems.at[tiles + i])
        for i, (a, b) in enumerate(
            ((degree_hbm, degree_ref), (known_hbm, known_ref), (y_hbm, y_ref))
        )
    ]
    copies = load_tiles(dense_hbm, dense_ref, tiles, sems, 0)
    for side in sides:
        side.wait()
    columns = degree_columns(degree_ref)
    outs = []
    for tile in range(tiles):
        rows = slice(tile * size, (tile + 1) * size)
        near = pl.ds(tile * size, size)
        copies[tile].wait()
        product = dot(dense_ref[rows, :], known_ref[...])
        base_ref[rows, :] = y_ref[rows, :].astype(F32) + DAMPING * scale_tile(
            columns, tile * size // block, product
        )
        outs.append(start(base_ref.at[near], base_hbm.at[near], sems.at[tile]))
    for out in outs:
        out.wait()


def final_kernel(
    degree_hbm, base_hbm, far_hbm, lu_hbm, ll_hbm, upper_ref, own_ref, sib_ref, low_ref,
    out_hbm,
    degree_ref, left_ref, coef_ref, stage_ref, sems,
):
    tiles = 4
    rank = lu_hbm.shape[1]
    block = degree_ref.shape[1]
    size = stage_ref.shape[0] // tiles
    degree_copy = start(degree_hbm, degree_ref, sems.at[0])
    sides = [
        start(far_hbm, left_ref.at[:, pl.ds(0, 2 * rank)], sems.at[1]),
        start(lu_hbm, left_ref.at[:, pl.ds(2 * rank, rank)], sems.at[2]),
        start(ll_hbm, left_ref.at[:, pl.ds(3 * rank, rank)], sems.at[3]),
    ]
    copies = load_tiles(base_hbm, stage_ref, tiles, sems, 4)
    parts, height, _ = upper_ref.shape
    lines = rank // parts
    width = (height - lines) // 3
    cols = parts * width
    whole = upper_ref[...]
    own_first = whole[:, :width].reshape(cols, rank)
    first = whole[:, width : 2 * width].reshape(cols, rank)
    second = whole[:, 2 * width : 3 * width].reshape(cols, rank)
    across = whole[:, 3 * width :].reshape(rank, rank)
    second = second + dot(own_first.astype(BF16), (DAMPING * across).astype(BF16))
    down = (DAMPING * low_ref[cols:, :]).astype(BF16)
    lower = (
        low_ref[:cols, :]
        + dot(first.astype(BF16), down[:rank])
        + dot(own_ref[...].astype(BF16), down[rank:])
    )
    coef_ref[:, 0 * rank : 1 * rank] = (DAMPING * first).astype(BF16)
    coef_ref[:, 1 * rank : 2 * rank] = (DAMPING * sib_ref[...]).astype(BF16)
    coef_ref[:, 2 * rank : 3 * rank] = (DAMPING * second).astype(BF16)
    coef_ref[:, 3 * rank : 4 * rank] = (DAMPING * lower).astype(BF16)
    degree_copy.wait()
    columns = degree_columns(degree_ref)
    for side in sides:
        side.wait()
    outs = []
    for tile in range(tiles):
        rows = slice(tile * size, (tile + 1) * size)
        near = pl.ds(tile * size, size)
        product = lax.dot_general(
            left_ref[rows, :], coef_ref[...], (((1,), (1,)), ((), ())), preferred_element_type=F32
        )
        copies[tile].wait()
        stage_ref[rows, :] = stage_ref[rows, :] + scale_tile(
            columns, tile * size // block, product
        )
        outs.append(start(stage_ref.at[near], out_hbm.at[near], sems.at[4 + tile]))
    for out in outs:
        out.wait()


def partner(value, axis, bit):
    pairs = [(source, source ^ (1 << bit)) for source in range(lax.axis_size(axis))]
    return lax.ppermute(value, axis, pairs)


def body(
    queries,
    inv_sqrt_degree,
    leaf_blocks,
    block_cols,
    left_upper,
    right_upper,
    left_lower,
    right_lower,
):
    inner_bits = lax.axis_size("inner").bit_length() - 1
    parts = lax.axis_size("inner") * lax.axis_size("mid")
    rows, cols = queries.shape
    rank = left_upper.shape[1]
    leaves, stored, block, _ = leaf_blocks.shape
    degree = inv_sqrt_degree.reshape(leaves, block)
    width, lines = cols // parts, rank // parts
    height = 2 * width + lines
    dma = pltpu.SemaphoreType.DMA
    degree_scratch = pltpu.VMEM((leaves, block), F32)

    def scratch(*dims):
        return pltpu.VMEM(dims, BF16)

    spread, right, late, early = call(
        coupling_kernel,
        [(degree, FAR), (left_upper, FAR), (left_lower, FAR), (right_upper, FAR), (right_lower, FAR)],
        [
            shape((rows, 2 * rank), BF16),
            shape((rows, 2 * rank), BF16),
            shape((3 * rank, rank), F32),
            shape((rank, rank), F32, True),
        ],
        [degree_scratch]
        + [scratch(rows, rank)] * 4
        + [scratch(rows, 2 * rank)] * 2
        + [pltpu.VMEM((3 * rank, rank), F32), dma((8,))],
        12,
        8 * rows * rank * rank,
    )
    for bit in range(inner_bits - 1):
        early = early + partner(early, "inner", bit)
    cross = partner(early, "inner", inner_bits - 1)

    scaled, coef, first_lower = call(
        first_kernel,
        [(degree, FAR), (queries, FAR), (right_upper, FAR), (right_lower, FAR)],
        [
            shape((rows, cols), BF16),
            shape((cols, 2 * rank), F32),
            shape((cols, rank), F32, True),
        ],
        [degree_scratch, scratch(rows, cols), scratch(rows, 2 * rank), scratch(rows, cols)]
        + [pltpu.VMEM((cols, 2 * rank), F32), dma((11,))],
        12,
        4 * rows * cols * rank,
    )
    own_lower = first_lower
    for bit in range(inner_bits - 1):
        own_lower = own_lower + partner(own_lower, "inner", bit)
    sib_lower = partner(own_lower, "inner", inner_bits - 1)

    dense, low, both = call(
        dense_kernel,
        [(block_cols, SMEM), (leaf_blocks, FAR), (scaled, FAR), (right, FAR), (coef, FAR), (late, FAR), (cross, VMEM)],
        [
            shape((rows, rows), BF16),
            shape((cols + 2 * rank, rank), F32),
            shape((parts, height, rank), F32, True),
        ],
        [scratch(leaves, stored, block, block), scratch(rows, rows), scratch(rows, cols), scratch(rows, 2 * rank)]
        + [pltpu.VMEM((cols, 2 * rank), F32), pltpu.VMEM((3 * rank, rank), F32)]
        + [pltpu.VMEM((cols + 2 * rank, rank), F32), dma((leaves + 4,))],
        36,
        4 * rows * rows * rank,
    )
    both = lax.all_to_all(both, ("mid", "inner"), 0, 0, tiled=True)

    known, far = call(
        known_kernel,
        [(degree, FAR), (dense, FAR), (scaled, FAR), (spread, FAR), (queries, FAR)],
        [shape((rows, cols), BF16), shape((rows, 2 * rank), BF16)],
        [degree_scratch, scratch(rows, rows), scratch(rows, cols), scratch(rows, 2 * rank)]
        + [scratch(rows, cols), scratch(rows, cols), scratch(rows, 2 * rank), dma((16,))],
        28,
        2 * rows * rows * (cols + 2 * rank),
    )
    both, known, far = lax.optimization_barrier((both, known, far))
    both = both.sum(axis=0)
    received = partner(both, "node", 0)
    sib = jnp.concatenate([both[:width], received], axis=0)
    sib = jnp.broadcast_to(sib[None], (parts,) + sib.shape)
    sib = lax.all_to_all(sib, ("mid", "inner"), 0, 0, tiled=True)

    for bit in range(inner_bits - 1):
        low = low + partner(low, "inner", bit)
    low = partner(low, "inner", inner_bits - 1)

    received, known = lax.optimization_barrier((received, known))
    (base,) = call(
        base_kernel,
        [(degree, FAR), (dense, FAR), (known, FAR), (queries, FAR)],
        [shape((rows, cols), F32)],
        [degree_scratch, scratch(rows, rows), scratch(rows, cols), scratch(rows, cols)]
        + [pltpu.VMEM((rows, cols), F32), dma((11,))],
        28,
        2 * rows * rows * cols,
    )

    (out,) = call(
        final_kernel,
        [(degree, FAR), (base, FAR), (far, FAR), (left_upper, FAR), (left_lower, FAR)]
        + [(sib, VMEM), (own_lower, VMEM), (sib_lower, VMEM), (low, VMEM)],
        [shape((rows, cols), F32)],
        [degree_scratch, scratch(rows, 4 * rank), scratch(cols, 4 * rank)]
        + [pltpu.VMEM((rows, cols), F32), dma((8,))],
        20,
        8 * rows * cols * rank,
    )
    return out


def solution(mesh):
    outer, inner = mesh.devices.shape
    fine = Mesh(mesh.devices.reshape(2, outer // 2, inner), ("node", "mid", "inner"))
    rows = P(("node", "mid", "inner"))
    return jax.shard_map(
        body, mesh=fine, in_specs=(rows,) * 8, out_specs=rows, check_vma=False
    )
```

time: 96.4 us -> 104 us (1.079)
  Pallas kernels: 0 us -> 47.1 us
  matrix products: 30.6 us -> 0 us
  waiting for transfers between devices: 46.8 us -> 33.7 us
  starting transfers between devices: 18.3 us -> 21.2 us
    pallas_call x0 -> x6, Pallas kernels: none -> 47.1 us  [call(): pl.pallas_call(kernel, out_shape=[out for out in outs], in_specs=[spec fo...]
    dot_general x11 -> x0, matrix products: 30.6 us -> none  [the longest x2 11.6 us: body(): leaf_term = jnp.dot(dense_leaf, scaled, preferred_element_type=jnp.float32)]
    ppermute x14 -> x7, waiting for transfers between devices: 46.8 us -> 33.7 us  [partner(): return lax.ppermute(value, axis, pairs)]
    all_to_all x0 -> x2, starting transfers between devices: none -> 9.19 us  [the longest x1 5.11 us: body(): sib = lax.all_to_all(sib, ('mid', 'inner'), 0, 0, tiled=True)]
    ppermute x14 -> x7, starting transfers between devices: 18.3 us -> 12 us  [partner(): return lax.ppermute(value, axis, pairs)]
  transfers between devices with their start and end apart: 14 -> 9, of which waited for: 8 -> 4; matrix products, arithmetic and copies ran while one was open for 23% -> 0% of each run, Pallas kernels for 0% -> 25%
where the time goes in v1:
time: 104 us; the launch traced here: 103 us
  Pallas kernels  47.1 us (45%)
  waiting for transfers between devices  33.7 us (32%)
  starting transfers between devices  21.2 us (20%)
    pallas_call x6, Pallas kernels, call(): pl.pallas_call(kernel, out_shape=[out for out in outs], in_specs=[spec fo...  47.1 us
    ppermute x7, waiting for transfers between devices, partner(): return lax.ppermute(value, axis, pairs)  33.7 us
    ppermute x7, starting transfers between devices, partner(): return lax.ppermute(value, axis, pairs)  12 us
    all_to_all x1, starting transfers between devices, body(): sib = lax.all_to_all(sib, ('mid', 'inner'), 0, 0, tiled=True)  5.11 us
    all_to_all x1, starting transfers between devices, body(): both = lax.all_to_all(both, ('mid', 'inner'), 0, 0, tiled=True)  4.08 us
  transfers between devices with their start and end apart: 9, of which 4 were waited for; matrix products, arithmetic and copies ran while one was open for 0% of the time, Pallas kernels for 25%

profile of v1, /device:TPU:0, one launch (start us, length us, event | category | flops | bytes accessed | tf_op | source)
XLA Modules:
  0.0 103.5 jit_solution(3461949526914767068)
XLA Ops:
  0.0 0.0 copy-start
  0.0 3.8 %shard_map.83 = (bf16[2048,256]{1,0:T(8,128)(2,1)}, bf16[2048,256]{1,0:T(8,128)(2,1)}, f32[384,128]{1,0:T(8,128)}, f32[128,128]{1,0:T(8,128)S(1)}) custom-call(f32[16,128]{1,0:T(8,128)} %bitcast.1, bf16[2048,128]{1,0:T(8,128)(2,1)} %lu_hbm.3, bf16[2048,128]{1,0:T(8,128)(2,1)} %ll_hbm.3, bf16[2048,128]{1,0:T(8,128)(2,1)} %ru_hbm.3, bf16[2048,128]{1,0:T(8,128)(2,1)} %rl_hbm.3), custom_call_target="tpu_custom_call" | custom-call | flops 268435456 | bytes 1048576 | tf_op jit(solution)/shard_map/pallas_call | solution.py:26
  3.8 3.0 %collective-permute-start = (f32[128,128]{1,0:T(8,128)S(1)}, f32[128,128]{1,0:T(8,128)S(1)}, u32[]{:S(2)}, u32[]{:S(2)}) collective-permute-start(f32[128,128]{1,0:T(8,128)S(1)} %get-tuple-element.25), channel_id=1, source_target_pairs={{0,1},{1,0},{2,3},{3,2},{4,5},{5,4},{6,7},{7,6},{8,9},{9,8},{10,11... | collective-permute-start | bytes 196616 | tf_op jit(solution)/shard_map/ppermute | solution.py:330
  6.8 2.2 %collective-permute-done = f32[128,128]{1,0:T(8,128)S(1)} collective-permute-done((f32[128,128]{1,0:T(8,128)S(1)}, f32[128,128]{1,0:T(8,128)S(1)}, u32[]{:S(2)}, u32[]{:S(2)}) %collective-permute-start) | collective-permute-done | bytes 65568 | tf_op jit(solution)/shard_map/ppermute | solution.py:330
  9.1 2.1 %collective-permute-start.1 = (f32[128,128]{1,0:T(8,128)S(1)}, f32[128,128]{1,0:T(8,128)S(1)}, u32[]{:S(2)}, u32[]{:S(2)}) collective-permute-start(f32[128,128]{1,0:T(8,128)S(1)} %add.9), channel_id=1, source_target_pairs={{0,2},{1,3},{2,0},{3,1},{4,6},{5,7},{6,4},{7,5},{8,10},{9,11},{10,... | collective-permute-start | bytes 196616 | tf_op jit(solution)/shard_map/ppermute | solution.py:330
  11.2 3.5 %shard_map.82 = (bf16[2048,512]{1,0:T(8,128)(2,1)}, f32[512,256]{1,0:T(8,128)}, f32[512,128]{1,0:T(8,128)S(1)}) custom-call(f32[16,128]{1,0:T(8,128)} %bitcast.2, bf16[2048,512]{1,0:T(8,128)(2,1)} %y_hbm.5, bf16[2048,128]{1,0:T(8,128)(2,1)} %ru_hbm.3, bf16[2048,128]{1,0:T(8,128)(2,1)} %rl_hbm.3), custom_call_target="tpu_custom_call" | custom-call | flops 536870912 | bytes 1048576 | tf_op jit(solution)/shard_map/pallas_call | solution.py:26
  14.7 0.0 collective-permute-done.1.cross_ref
  14.7 0.0 copy-done
  14.7 12.2 %shard_map.84 = (bf16[2048,2048]{1,0:T(8,128)(2,1)}, f32[768,128]{1,0:T(8,128)}, f32[16,72,128]{2,1,0:T(8,128)}) custom-call(s32[16,12]{1,0:T(8,128)S(1)} %copy-done, bf16[16,12,128,128]{3,2,1,0:T(8,128)(2,1)} %blocks_hbm.1, bf16[2048,512]{1,0:T(8,128)(2,1)} %get-tuple-element.21.scaled_hbm, bf16[2048,256]{1,0:T(8,128)(2,1)} %get-tuple-element.22.right_hbm, ...), custom_call_target="tpu_custom_call" | custom-call | flops 2147483648 | bytes 1048576 | tf_op jit(solution)/shard_map/pallas_call | solution.py:26
  26.9 4.1 %all-to-all-start = ((f32[16,72,128]{2,1,0:T(8,128)}), f32[16,72,128]{2,1,0:T(8,128)S(1)}, u32[]{:S(2)}, u32[]{:S(2)}) async-start(f32[16,72,128]{2,1,0:T(8,128)} %get-tuple-element.27), calls=%async_computation | async-start | bytes 1179648 | tf_op jit(solution)/shard_map/all_to_all | solution.py:409
  31.0 0.0 copy-start.1
  31.0 13.7 %shard_map.85 = (bf16[2048,512]{1,0:T(8,128)(2,1)}, bf16[2048,256]{1,0:T(8,128)(2,1)}) custom-call(f32[16,128]{1,0:T(8,128)} %bitcast.3, bf16[2048,2048]{1,0:T(8,128)(2,1)} %get-tuple-element.26.dense_hbm, bf16[2048,512]{1,0:T(8,128)(2,1)} %get-tuple-element.21.scaled_hbm, bf16[2048,256]{1,0:T(8,128)(2,1)} %get-tuple-element.28.spread_hbm, ...), custom_call_target="tpu_custom_call" | custom-call | flops 6442450944 | bytes 1048576 | tf_op jit(solution)/shard_map/pallas_call | solution.py:26
  44.7 0.0 all-to-all-done
  44.8 2.7 %collective-permute-start.2 = (f32[72,128]{1,0:T(8,128)S(1)}, f32[72,128]{1,0:T(8,128)S(1)}, u32[]{:S(2)}, u32[]{:S(2)}) collective-permute-start(f32[72,128]{1,0:T(8,128)S(1)} %reduce_sum.9), channel_id=1, source_target_pairs={{0,16},{16,0},{1,17},{17,1},{2,18},{18,2},{3,19},{19,3},{4,20},{20... | collective-permute-start | bytes 110600 | tf_op jit(solution)/shard_map/ppermute | solution.py:330
  47.4 2.3 %collective-permute-done.2 = f32[72,128]{1,0:T(8,128)S(1)} collective-permute-done((f32[72,128]{1,0:T(8,128)S(1)}, f32[72,128]{1,0:T(8,128)S(1)}, u32[]{:S(2)}, u32[]{:S(2)}) %collective-permute-start.2) | collective-permute-done | bytes 36896 | tf_op jit(solution)/shard_map/ppermute | solution.py:330
  49.7 1.0 broadcast_in_dim.2
  50.6 5.1 %all-to-all-start.1 = ((f32[16,104,128]{2,1,0:T(8,128)}), f32[16,104,128]{2,1,0:T(8,128)S(1)}, u32[]{:S(2)}, u32[]{:S(2)}) async-start(f32[16,104,128]{2,1,0:T(8,128)} %broadcast_in_dim.2), calls=%async_computation.1 | async-start | bytes 1703936 | tf_op jit(solution)/shard_map/all_to_all | solution.py:425
  55.8 0.0 copy-done.1
  55.8 2.0 %collective-permute-start.5 = (f32[768,128]{1,0:T(8,128)S(1)}, f32[768,128]{1,0:T(8,128)S(1)}, u32[]{:S(2)}, u32[]{:S(2)}) collective-permute-start(f32[768,128]{1,0:T(8,128)S(1)} %copy-done.1), channel_id=1, source_target_pairs={{0,1},{1,0},{2,3},{3,2},{4,5},{5,4},{6,7},{7,6},{8,9},{9,8},{10,11... | collective-permute-start | bytes 1179656 | tf_op jit(solution)/shard_map/ppermute | solution.py:330
  57.7 0.1 collective-permute-start.3
  57.9 24.2 %collective-permute-done.3 = f32[512,128]{1,0:T(8,128)S(1)} collective-permute-done((f32[512,128]{1,0:T(8,128)S(1)}, f32[512,128]{1,0:T(8,128)S(1)}, u32[]{:S(2)}, u32[]{:S(2)}) %collective-permute-start.3) | collective-permute-done | bytes 262176 | tf_op jit(solution)/shard_map/ppermute | solution.py:330
  82.1 1.5 %collective-permute-start.4 = (f32[512,128]{1,0:T(8,128)S(1)}, f32[512,128]{1,0:T(8,128)S(1)}, u32[]{:S(2)}, u32[]{:S(2)}) collective-permute-start(f32[512,128]{1,0:T(8,128)S(1)} %add.10.own_ref), channel_id=1, source_target_pairs={{0,2},{1,3},{2,0},{3,1},{4,6},{5,7},{6,4},{7,5},{8,10},{9,11},{10,... | collective-permute-start | bytes 786440 | tf_op jit(solution)/shard_map/ppermute | solution.py:330
  83.6 0.0 collective-permute-done.5
  83.6 0.1 add.11
  83.7 0.6 collective-permute-start.6
  84.3 9.1 %shard_map.86.base_hbm = f32[2048,512]{1,0:T(8,128)} custom-call(f32[16,128]{1,0:T(8,128)} %bitcast.4, bf16[2048,2048]{1,0:T(8,128)(2,1)} %get-tuple-element.26.dense_hbm, bf16[2048,512]{1,0:T(8,128)(2,1)} %get-tuple-element.33.known_hbm, bf16[2048,512]{1,0:T(8,128)(2,1)} %y_hbm.5), custom_call_target="tpu_custom_call" | custom-call | flops 4294967296 | bytes 1048576 | tf_op jit(solution)/shard_map/pallas_call | solution.py:26
  93.4 0.0 collective-permute-done.4.sib_ref
  93.4 5.0 %collective-permute-done.6.low_ref = f32[768,128]{1,0:T(8,128)S(1)} collective-permute-done((f32[768,128]{1,0:T(8,128)S(1)}, f32[768,128]{1,0:T(8,128)S(1)}, u32[]{:S(2)}, u32[]{:S(2)}) %collective-permute-start.6) | collective-permute-done | bytes 393248 | tf_op jit(solution)/shard_map/ppermute | solution.py:330
  98.4 0.0 all-to-all-done.1.upper_ref
  98.4 4.9 %shard_map.87 = f32[2048,512]{1,0:T(8,128)} custom-call(f32[16,128]{1,0:T(8,128)} %bitcast.5, f32[2048,512]{1,0:T(8,128)} %shard_map.86.base_hbm, bf16[2048,256]{1,0:T(8,128)(2,1)} %get-tuple-element.34.far_hbm, bf16[2048,128]{1,0:T(8,128)(2,1)} %lu_hbm.3, bf16[2048,128]{1,0:T(8,128)(2,1)} %ll_hbm.3, f32[16,104,128]{2,1,0:T(8,128)S(1)} %all-to-all-done.1.upper_ref, ...), custom_call_target="tpu_custom_call" | custom-call | flops 1073741824 | bytes 1048576 | tf_op jit(solution)/shard_map/pallas_call | solution.py:26
  (5 shorter events, 0.1 us)
Async XLA Ops:
  0.0 14.7 %copy-start = (s32[16,12]{1,0:T(8,128)S(1)}, s32[16,12]{1,0:T(8,128)}, u32[]{:S(2)}) copy-start(s32[16,12]{1,0:T(8,128)} %cols_ref.1) | copy-start | bytes 2308
  3.8 5.2 %collective-permute-start = (f32[128,128]{1,0:T(8,128)S(1)}, f32[128,128]{1,0:T(8,128)S(1)}, u32[]{:S(2)}, u32[]{:S(2)}) collective-permute-start(f32[128,128]{1,0:T(8,128)S(1)} %get-tuple-element.25), channel_id=1, source_target_pairs={{0,1},{1,0},{2,3},{3,2},{4,5},{5,4},{6,7},{7,6},{8,9},{9,8},{10,11... | collective-permute-start | bytes 196616 | tf_op jit(solution)/shard_map/ppermute | solution.py:330
  9.1 5.6 %collective-permute-start.1 = (f32[128,128]{1,0:T(8,128)S(1)}, f32[128,128]{1,0:T(8,128)S(1)}, u32[]{:S(2)}, u32[]{:S(2)}) collective-permute-start(f32[128,128]{1,0:T(8,128)S(1)} %add.9), channel_id=1, source_target_pairs={{0,2},{1,3},{2,0},{3,1},{4,6},{5,7},{6,4},{7,5},{8,10},{9,11},{10,... | collective-permute-start | bytes 196616 | tf_op jit(solution)/shard_map/ppermute | solution.py:330
  26.9 17.8 %all-to-all-start = ((f32[16,72,128]{2,1,0:T(8,128)}), f32[16,72,128]{2,1,0:T(8,128)S(1)}, u32[]{:S(2)}, u32[]{:S(2)}) async-start(f32[16,72,128]{2,1,0:T(8,128)} %get-tuple-element.27), calls=%async_computation | async-start | bytes 1179648 | tf_op jit(solution)/shard_map/all_to_all | solution.py:409
  31.0 24.8 %copy-start.1 = (f32[768,128]{1,0:T(8,128)S(1)}, f32[768,128]{1,0:T(8,128)}, u32[]{:S(2)}) copy-start(f32[768,128]{1,0:T(8,128)} %get-tuple-element.36) | copy-start | bytes 1179652
  44.8 4.9 %collective-permute-start.2 = (f32[72,128]{1,0:T(8,128)S(1)}, f32[72,128]{1,0:T(8,128)S(1)}, u32[]{:S(2)}, u32[]{:S(2)}) collective-permute-start(f32[72,128]{1,0:T(8,128)S(1)} %reduce_sum.9), channel_id=1, source_target_pairs={{0,16},{16,0},{1,17},{17,1},{2,18},{18,2},{3,19},{19,3},{4,20},{20... | collective-permute-start | bytes 110600 | tf_op jit(solution)/shard_map/ppermute | solution.py:330
  50.6 47.8 %all-to-all-start.1 = ((f32[16,104,128]{2,1,0:T(8,128)}), f32[16,104,128]{2,1,0:T(8,128)S(1)}, u32[]{:S(2)}, u32[]{:S(2)}) async-start(f32[16,104,128]{2,1,0:T(8,128)} %broadcast_in_dim.2), calls=%async_computation.1 | async-start | bytes 1703936 | tf_op jit(solution)/shard_map/all_to_all | solution.py:425
  55.8 27.9 %collective-permute-start.5 = (f32[768,128]{1,0:T(8,128)S(1)}, f32[768,128]{1,0:T(8,128)S(1)}, u32[]{:S(2)}, u32[]{:S(2)}) collective-permute-start(f32[768,128]{1,0:T(8,128)S(1)} %copy-done.1), channel_id=1, source_target_pairs={{0,1},{1,0},{2,3},{3,2},{4,5},{5,4},{6,7},{7,6},{8,9},{9,8},{10,11... | collective-permute-start | bytes 1179656 | tf_op jit(solution)/shard_map/ppermute | solution.py:330
  57.7 24.3 %collective-permute-start.3 = (f32[512,128]{1,0:T(8,128)S(1)}, f32[512,128]{1,0:T(8,128)S(1)}, u32[]{:S(2)}, u32[]{:S(2)}) collective-permute-start(f32[512,128]{1,0:T(8,128)S(1)} %get-tuple-element.35), channel_id=1, source_target_pairs={{0,1},{1,0},{2,3},{3,2},{4,5},{5,4},{6,7},{7,6},{8,9},{9,8},{10,11... | collective-permute-start | bytes 786440 | tf_op jit(solution)/shard_map/ppermute | solution.py:330
  82.1 11.3 %collective-permute-start.4 = (f32[512,128]{1,0:T(8,128)S(1)}, f32[512,128]{1,0:T(8,128)S(1)}, u32[]{:S(2)}, u32[]{:S(2)}) collective-permute-start(f32[512,128]{1,0:T(8,128)S(1)} %add.10.own_ref), channel_id=1, source_target_pairs={{0,2},{1,3},{2,0},{3,1},{4,6},{5,7},{6,4},{7,5},{8,10},{9,11},{10,... | collective-permute-start | bytes 786440 | tf_op jit(solution)/shard_map/ppermute | solution.py:330
  83.7 14.7 %collective-permute-start.6 = (f32[768,128]{1,0:T(8,128)S(1)}, f32[768,128]{1,0:T(8,128)S(1)}, u32[]{:S(2)}, u32[]{:S(2)}) collective-permute-start(f32[768,128]{1,0:T(8,128)S(1)} %add.11), channel_id=1, source_target_pairs={{0,2},{1,3},{2,0},{3,1},{4,6},{5,7},{6,4},{7,5},{8,10},{9,11},{10,... | collective-permute-start | bytes 1179656 | tf_op jit(solution)/shard_map/ppermute | solution.py:330

commit v2 on v1

v2 whole, which is shorter than its diff:
```python
import jax
import jax.numpy as jnp
from jax import lax
from jax.experimental import pallas as pl
from jax.experimental.pallas import tpu as pltpu
from jax.sharding import Mesh
from jax.sharding import PartitionSpec as P

DAMPING = 0.9
F32 = jnp.float32
BF16 = jnp.bfloat16
VMEM = pl.BlockSpec(memory_space=pltpu.VMEM)
SMEM = pl.BlockSpec(memory_space=pltpu.SMEM)
FAR = pl.BlockSpec(memory_space=pltpu.HBM)


def shape(dims, dtype, near=False):
    return (pltpu.VMEM if near else pltpu.HBM)(dims, dtype)


def call(kernel, args, outs, scratch, megabytes, flops):
    values = [
        value if spec is SMEM else pltpu.with_memory_space_constraint(value, spec.memory_space)
        for value, spec in args
    ]
    return pl.pallas_call(
        kernel,
        out_shape=[out for out in outs],
        in_specs=[spec for _, spec in args],
        out_specs=[
            FAR if out.memory_space == pltpu.HBM else VMEM for out in outs
        ],
        scratch_shapes=scratch,
        cost_estimate=pl.CostEstimate(
            flops=flops, bytes_accessed=2**20, transcendentals=0
        ),
        compiler_params=pltpu.CompilerParams(vmem_limit_bytes=megabytes * 2**20),
    )(*values)


def dot(a, b):
    return jnp.dot(a, b, preferred_element_type=F32)


def tdot(a, b):
    return lax.dot_general(a, b, (((0,), (0,)), ((), ())), preferred_element_type=F32)


def start(source, target, sem):
    copy = pltpu.make_async_copy(source, target, sem)
    copy.start()
    return copy


def degree_columns(degree_ref):
    leaves, block = degree_ref.shape
    tall = jnp.concatenate([degree_ref[...]] * (block // leaves), axis=0)
    return tall.T[:, :leaves]


def scale_tile(columns, first, value):
    block = columns.shape[0]
    return jnp.concatenate(
        [
            columns[:, first + b : first + b + 1] * value[b * block : (b + 1) * block]
            for b in range(value.shape[0] // block)
        ],
        axis=0,
    )


def first_kernel(
    degree_hbm, y_hbm, lu_hbm, ll_hbm, ru_hbm, rl_hbm,
    coef_hbm, coupling_hbm, lower_ref,
    degree_ref, y_ref, left_ref, right_ref, scaled_ref, spread_ref, coef_ref, coupling_ref, sems,
):
    leaves, block = degree_ref.shape
    rank = ru_hbm.shape[1]
    upper, lower = pl.ds(0, rank), pl.ds(rank, rank)
    copies = [start(degree_hbm, degree_ref, sems.at[0])]
    for i, (a, b) in enumerate(
        (
            (ll_hbm, left_ref.at[:, lower]),
            (ru_hbm, right_ref.at[:, upper]),
            (rl_hbm, right_ref.at[:, lower]),
            (lu_hbm, left_ref.at[:, upper]),
        )
    ):
        copies.append(start(a, b, sems.at[1 + i]))
    tiles = 4
    loads = load_tiles(y_hbm, y_ref, tiles, sems, 5)
    size = y_ref.shape[0] // tiles
    for copy in copies:
        copy.wait()
    columns = degree_columns(degree_ref)
    square = columns * columns
    for leaf in range(leaves):
        rows = slice(leaf * block, (leaf + 1) * block)
        spread_ref[rows, :] = scale_tile(square, leaf, left_ref[rows, :].astype(F32)).astype(BF16)
    coupling_ref[...] = tdot(spread_ref[...], right_ref[...])
    outs = [start(coupling_ref, coupling_hbm, sems.at[0])]
    for tile in range(tiles):
        loads[tile].wait()
        rows = slice(tile * size, (tile + 1) * size)
        value = y_ref[rows, :].astype(F32)
        scaled_ref[rows, :] = scale_tile(columns, tile * size // block, value).astype(BF16)
    coef_ref[...] = tdot(scaled_ref[...], right_ref[...])
    outs.append(start(coef_ref, coef_hbm, sems.at[1]))
    for slot in range(lower_ref.shape[0]):
        lower_ref[slot] = coef_ref[:, rank:]
    for out in outs:
        out.wait()


def load_tiles(hbm, ref, tiles, sems, first):
    size = ref.shape[0] // tiles
    return [
        start(hbm.at[pl.ds(t * size, size)], ref.at[pl.ds(t * size, size)], sems.at[first + t])
        for t in range(tiles)
    ]


def load_blocks(blocks_hbm, blocks_ref, sems, first):
    return [
        start(blocks_hbm.at[row], blocks_ref.at[row], sems.at[first + row])
        for row in range(blocks_ref.shape[0])
    ]


def place(cols_ref, copies, blocks_ref, dense_ref):
    leaves, stored, block, _ = blocks_ref.shape
    for row in range(leaves):
        rows = slice(row * block, (row + 1) * block)
        dense_ref[rows, :] = jnp.zeros((block, leaves * block), BF16)
        copies[row].wait()
        for j in range(stored):
            col = pl.multiple_of(cols_ref[row, j] * block, block)
            dense_ref[rows, pl.ds(col, block)] = blocks_ref[row, j]


def known_kernel(
    cols_ref, degree_hbm, blocks_hbm, y_hbm, ru_hbm, rl_hbm, coef_hbm, coupling_hbm,
    known_hbm, both_ref, low_ref, lower_coupling_ref,
    degree_ref, blocks_ref, dense_ref, y_ref, scaled_ref, known_ref, right_ref, coef_ref, coupling_ref, sems,
):
    leaves, _, block, _ = blocks_ref.shape
    rank = ru_hbm.shape[1]
    tiles = 4
    size = y_ref.shape[0] // tiles
    degree_copy = start(degree_hbm, degree_ref, sems.at[leaves])
    loads = load_tiles(y_hbm, y_ref, tiles, sems, leaves + 1)
    copies = load_blocks(blocks_hbm, blocks_ref, sems, 0)
    sides = [
        start(ru_hbm, right_ref.at[:, pl.ds(0, rank)], sems.at[leaves + 5]),
        start(rl_hbm, right_ref.at[:, pl.ds(rank, rank)], sems.at[leaves + 6]),
        start(coef_hbm, coef_ref, sems.at[leaves + 7]),
        start(coupling_hbm, coupling_ref, sems.at[leaves + 8]),
    ]
    place(cols_ref, copies, blocks_ref, dense_ref)
    degree_copy.wait()
    columns = degree_columns(degree_ref)
    for tile in range(tiles):
        loads[tile].wait()
        rows = slice(tile * size, (tile + 1) * size)
        value = y_ref[rows, :].astype(F32)
        scaled_ref[rows, :] = scale_tile(columns, tile * size // block, value).astype(BF16)
    for side in sides:
        side.wait()
    outs = []
    for tile in range(tiles):
        rows = slice(tile * size, (tile + 1) * size)
        near = pl.ds(tile * size, size)
        first = tile * size // block
        product = dot(dense_ref[rows, :], scaled_ref[...])
        value = y_ref[rows, :].astype(F32) + DAMPING * scale_tile(columns, first, product)
        known_ref[rows, :] = scale_tile(columns, first, value).astype(BF16)
        outs.append(start(known_ref.at[near], known_hbm.at[near], sems.at[tile]))
    found = tdot(known_ref[...], right_ref[...])
    low_ref[: found.shape[0], :] = found[:, rank:]
    low_ref[found.shape[0] :, :] = coupling_ref[:rank, rank:]
    lower_coupling_ref[...] = coupling_ref[rank:, :]
    parts, height, _ = both_ref.shape
    width = found.shape[0] // parts
    lines = rank // parts
    both_ref[:, :width, :] = coef_ref[:, :rank].reshape(parts, width, rank)
    both_ref[:, width : 2 * width, :] = found[:, :rank].reshape(parts, width, rank)
    for part in range(parts):
        both_ref[part, 2 * width : 2 * width + lines, :] = coupling_ref[
            part * lines : (part + 1) * lines, :rank
        ]
    for out in outs:
        out.wait()


def pack_kernel(
    half_ref, gathered_ref, both_in_ref, low_in_ref, coupling_ref,
    both_ref, low_ref, sib_hbm,
    sib_ref, sem,
):
    count = gathered_ref.shape[0] // 2
    first = (1 - half_ref[0]) * count
    sib = gathered_ref[first]
    for i in range(1, count):
        sib = sib + gathered_ref[first + i]
    sib_ref[...] = sib
    out = start(sib_ref, sib_hbm, sem)
    cols, rank = sib.shape
    update = dot((DAMPING * sib).astype(BF16), coupling_ref[...].astype(BF16))
    parts, height, _ = both_ref.shape
    width = cols // parts
    both_ref[...] = both_in_ref[...]
    both_ref[:, width : 2 * width, :] = both_in_ref[:, width : 2 * width, :] + update[
        :, :rank
    ].reshape(parts, width, rank)
    low_ref[:cols, :] = low_in_ref[:cols, :] + update[:, rank:]
    low_ref[cols:, :] = low_in_ref[cols:, :]
    out.wait()


def far_kernel(
    cols_ref, degree_hbm, blocks_hbm, lu_hbm, ll_hbm,
    far_hbm,
    degree_ref, blocks_ref, dense_ref, left_ref, spread_ref, far_ref, sems,
):
    leaves, _, block, _ = blocks_ref.shape
    rank = lu_hbm.shape[1]
    sides = [
        start(degree_hbm, degree_ref, sems.at[leaves]),
        start(lu_hbm, left_ref.at[:, pl.ds(0, rank)], sems.at[leaves + 1]),
        start(ll_hbm, left_ref.at[:, pl.ds(rank, rank)], sems.at[leaves + 2]),
    ]
    copies = load_blocks(blocks_hbm, blocks_ref, sems, 0)
    for side in sides:
        side.wait()
    columns = degree_columns(degree_ref)
    square = columns * columns
    for leaf in range(leaves):
        rows = slice(leaf * block, (leaf + 1) * block)
        spread_ref[rows, :] = scale_tile(square, leaf, left_ref[rows, :].astype(F32)).astype(BF16)
    place(cols_ref, copies, blocks_ref, dense_ref)
    far_ref[...] = (DAMPING * dot(dense_ref[...], spread_ref[...])).astype(BF16)
    start(far_ref, far_hbm, sems.at[0]).wait()


def base_kernel(
    cols_ref, degree_hbm, blocks_hbm, known_hbm, y_hbm,
    base_hbm,
    degree_ref, blocks_ref, dense_ref, known_ref, y_ref, base_ref, sems,
):
    leaves, _, block, _ = blocks_ref.shape
    copies = load_blocks(blocks_hbm, blocks_ref, sems, 0)
    sides = [
        start(a, b, sems.at[leaves + i])
        for i, (a, b) in enumerate(
            ((degree_hbm, degree_ref), (known_hbm, known_ref), (y_hbm, y_ref))
        )
    ]
    place(cols_ref, copies, blocks_ref, dense_ref)
    for side in sides:
        side.wait()
    columns = degree_columns(degree_ref)
    tiles = 4
    size = y_ref.shape[0] // tiles
    outs = []
    for tile in range(tiles):
        rows = slice(tile * size, (tile + 1) * size)
        near = pl.ds(tile * size, size)
        product = dot(dense_ref[rows, :], known_ref[...])
        base_ref[rows, :] = y_ref[rows, :].astype(F32) + DAMPING * scale_tile(
            columns, tile * size // block, product
        )
        outs.append(start(base_ref.at[near], base_hbm.at[near], sems.at[tile]))
    for out in outs:
        out.wait()


def final_kernel(
    degree_hbm, base_hbm, far_hbm, lu_hbm, ll_hbm, sib_hbm, upper_ref, low_ref,
    out_hbm,
    degree_ref, left_ref, coef_ref, sib_ref, stage_ref, sems,
):
    tiles = 4
    rank = lu_hbm.shape[1]
    block = degree_ref.shape[1]
    size = stage_ref.shape[0] // tiles
    degree_copy = start(degree_hbm, degree_ref, sems.at[0])
    sib_copy = start(sib_hbm, sib_ref, sems.at[8])
    sides = [
        start(far_hbm, left_ref.at[:, pl.ds(0, 2 * rank)], sems.at[1]),
        start(lu_hbm, left_ref.at[:, pl.ds(2 * rank, rank)], sems.at[2]),
        start(ll_hbm, left_ref.at[:, pl.ds(3 * rank, rank)], sems.at[3]),
    ]
    copies = load_tiles(base_hbm, stage_ref, tiles, sems, 4)
    parts, height, _ = upper_ref.shape
    lines = rank // parts
    width = (height - lines) // 3
    cols = parts * width
    whole = upper_ref[...]
    own_first = whole[:, :width].reshape(cols, rank)
    first = whole[:, width : 2 * width].reshape(cols, rank)
    second = whole[:, 2 * width : 3 * width].reshape(cols, rank)
    across = whole[:, 3 * width :].reshape(rank, rank)
    second = second + dot(own_first.astype(BF16), (DAMPING * across).astype(BF16))
    down = (DAMPING * low_ref[cols:, :]).astype(BF16)
    lower = low_ref[:cols, :] + dot(first.astype(BF16), down)
    sib_copy.wait()
    coef_ref[:, 0 * rank : 1 * rank] = (DAMPING * first).astype(BF16)
    coef_ref[:, 1 * rank : 2 * rank] = (DAMPING * sib_ref[...]).astype(BF16)
    coef_ref[:, 2 * rank : 3 * rank] = (DAMPING * second).astype(BF16)
    coef_ref[:, 3 * rank : 4 * rank] = (DAMPING * lower).astype(BF16)
    degree_copy.wait()
    columns = degree_columns(degree_ref)
    for side in sides:
        side.wait()
    outs = []
    for tile in range(tiles):
        rows = slice(tile * size, (tile + 1) * size)
        near = pl.ds(tile * size, size)
        product = lax.dot_general(
            left_ref[rows, :], coef_ref[...], (((1,), (1,)), ((), ())), preferred_element_type=F32
        )
        copies[tile].wait()
        stage_ref[rows, :] = stage_ref[rows, :] + scale_tile(
            columns, tile * size // block, product
        )
        outs.append(start(stage_ref.at[near], out_hbm.at[near], sems.at[4 + tile]))
    for out in outs:
        out.wait()


def partner(value, axis, bit):
    pairs = [(source, source ^ (1 << bit)) for source in range(lax.axis_size(axis))]
    return lax.ppermute(value, axis, pairs)


def body(
    queries,
    inv_sqrt_degree,
    leaf_blocks,
    block_cols,
    left_upper,
    right_upper,
    left_lower,
    right_lower,
):
    inner_bits = lax.axis_size("inner").bit_length() - 1
    parts = lax.axis_size("inner") * lax.axis_size("mid")
    rows, cols = queries.shape
    rank = left_upper.shape[1]
    leaves, stored, block, _ = leaf_blocks.shape
    degree = inv_sqrt_degree.reshape(leaves, block)
    width, lines = cols // parts, rank // parts
    height = 2 * width + lines
    dma = pltpu.SemaphoreType.DMA
    degree_scratch = pltpu.VMEM((leaves, block), F32)

    def scratch(*dims):
        return pltpu.VMEM(dims, BF16)

    near_f32 = lambda *dims: pltpu.VMEM(dims, F32)
    inner = lax.axis_size("inner")
    coef, coupling, gathered = call(
        first_kernel,
        [(degree, FAR), (queries, FAR), (left_upper, FAR), (left_lower, FAR), (right_upper, FAR), (right_lower, FAR)],
        [
            shape((cols, 2 * rank), F32),
            shape((2 * rank, 2 * rank), F32),
            shape((inner, cols, rank), F32, True),
        ],
        [degree_scratch, scratch(rows, cols), scratch(rows, 2 * rank), scratch(rows, 2 * rank)]
        + [scratch(rows, cols), scratch(rows, 2 * rank), near_f32(cols, 2 * rank)]
        + [near_f32(2 * rank, 2 * rank), dma((9,))],
        14,
        4 * rows * (cols + 2 * rank) * rank,
    )
    gathered = lax.all_to_all(gathered, "inner", 0, 0, tiled=True)

    known, both, low, lower_coupling = call(
        known_kernel,
        [(block_cols, SMEM), (degree, FAR), (leaf_blocks, FAR), (queries, FAR), (right_upper, FAR), (right_lower, FAR)]
        + [(coef, FAR), (coupling, FAR)],
        [
            shape((rows, cols), BF16),
            shape((parts, height, rank), F32, True),
            shape((cols + rank, rank), F32, True),
            shape((rank, 2 * rank), F32, True),
        ],
        [degree_scratch, scratch(leaves, stored, block, block), scratch(rows, rows), scratch(rows, cols)]
        + [scratch(rows, cols), scratch(rows, cols), scratch(rows, 2 * rank), near_f32(cols, 2 * rank)]
        + [near_f32(2 * rank, 2 * rank), dma((leaves + 9,))],
        36,
        2 * rows * rows * cols,
    )
    half = (lax.axis_index("inner") // (inner // 2)).astype(jnp.int32).reshape(1)
    both, low, sib_lower = call(
        pack_kernel,
        [(half, SMEM), (gathered, VMEM), (both, VMEM), (low, VMEM), (lower_coupling, VMEM)],
        [
            shape((parts, height, rank), F32, True),
            shape((cols + rank, rank), F32, True),
            shape((cols, rank), F32),
        ],
        [near_f32(cols, rank), dma(())],
        8,
        4 * cols * rank * rank,
    )
    both = lax.all_to_all(both, ("mid", "inner"), 0, 0, tiled=True)

    (far,) = call(
        far_kernel,
        [(block_cols, SMEM), (degree, FAR), (leaf_blocks, FAR), (left_upper, FAR), (left_lower, FAR)],
        [shape((rows, 2 * rank), BF16)],
        [degree_scratch, scratch(leaves, stored, block, block), scratch(rows, rows)]
        + [scratch(rows, 2 * rank)] * 3
        + [dma((leaves + 3,))],
        26,
        4 * rows * rows * rank,
    )
    both, far = lax.optimization_barrier((both, far))
    both = both.sum(axis=0)
    received = partner(both, "node", 0)
    for bit in range(inner_bits - 1):
        low = low + partner(low, "inner", bit)
    received, low, known = lax.optimization_barrier((received, low, known))
    low = partner(low, "inner", inner_bits - 1)
    sib = jnp.concatenate([both[:width], received], axis=0)
    sib = jnp.broadcast_to(sib[None], (parts,) + sib.shape)
    sib = lax.all_to_all(sib, ("mid", "inner"), 0, 0, tiled=True)


    (base,) = call(
        base_kernel,
        [(block_cols, SMEM), (degree, FAR), (leaf_blocks, FAR), (known, FAR), (queries, FAR)],
        [shape((rows, cols), F32)],
        [degree_scratch, scratch(leaves, stored, block, block), scratch(rows, rows)]
        + [scratch(rows, cols)] * 2
        + [near_f32(rows, cols), dma((leaves + 3,))],
        32,
        2 * rows * rows * cols,
    )

    (out,) = call(
        final_kernel,
        [(degree, FAR), (base, FAR), (far, FAR), (left_upper, FAR), (left_lower, FAR)]
        + [(sib_lower, FAR), (sib, VMEM), (low, VMEM)],
        [shape((rows, cols), F32)],
        [degree_scratch, scratch(rows, 4 * rank), scratch(cols, 4 * rank)]
        + [near_f32(cols, rank), near_f32(rows, cols), dma((9,))],
        20,
        8 * rows * cols * rank,
    )
    return out


def solution(mesh):
    outer, inner = mesh.devices.shape
    fine = Mesh(mesh.devices.reshape(2, outer // 2, inner), ("node", "mid", "inner"))
    rows = P(("node", "mid", "inner"))
    return jax.shard_map(
        body, mesh=fine, in_specs=(rows,) * 8, out_specs=rows, check_vma=False
    )
```

time: 104 us -> 76.4 us (0.73)
  waiting for transfers between devices: 33.7 us -> 12.8 us
  Pallas kernels: 47.1 us -> 42.5 us
  starting transfers between devices: 21.2 us -> 19.4 us
    ppermute x7 -> x3, waiting for transfers between devices: 33.7 us -> 10.6 us  [partner(): return lax.ppermute(value, axis, pairs)]
    ppermute x7 -> x3, starting transfers between devices: 12 us -> 6.56 us  [partner(): return lax.ppermute(value, axis, pairs)]
    all_to_all x0 -> x1, starting transfers between devices: none -> 5.18 us  [body(): gathered = lax.all_to_all(gathered, 'inner', 0, 0, tiled=True)]
    pallas_call x6, Pallas kernels: 47.1 us -> 42.5 us  [call(): pl.pallas_call(kernel, out_shape=[out for out in outs], in_specs=[spec fo...]
    all_to_all x0 -> x1, waiting for transfers between devices: none -> 2.17 us  [body(): gathered = lax.all_to_all(gathered, 'inner', 0, 0, tiled=True)]
    all_to_all x1, starting transfers between devices: 5.11 us -> 3.75 us  [body(): sib = lax.all_to_all(sib, ('mid', 'inner'), 0, 0, tiled=True)]
  transfers between devices with their start and end apart: 9 -> 6, of which waited for: 4 -> 3; matrix products, arithmetic and copies ran while one was open for 0% -> 0% of each run, Pallas kernels for 25% -> 39%
where the time goes in v2:
time: 76.4 us; the launch traced here: 76.1 us
  Pallas kernels  42.5 us (56%)
  starting transfers between devices  19.4 us (25%)
  waiting for transfers between devices  12.8 us (17%)
  local copies, waits for them, and re-layouts  1.01 us (1%)
    pallas_call x6, Pallas kernels, call(): pl.pallas_call(kernel, out_shape=[out for out in outs], in_specs=[spec fo...  42.5 us
    ppermute x3, waiting for transfers between devices, partner(): return lax.ppermute(value, axis, pairs)  10.6 us
    ppermute x3, starting transfers between devices, partner(): return lax.ppermute(value, axis, pairs)  6.56 us
    all_to_all x1, starting transfers between devices, body(): gathered = lax.all_to_all(gathered, 'inner', 0, 0, tiled=True)  5.18 us
    all_to_all x1, starting transfers between devices, body(): both = lax.all_to_all(both, ('mid', 'inner'), 0, 0, tiled=True)  3.93 us
    all_to_all x1, starting transfers between devices, body(): sib = lax.all_to_all(sib, ('mid', 'inner'), 0, 0, tiled=True)  3.75 us
    all_to_all x1, waiting for transfers between devices, body(): gathered = lax.all_to_all(gathered, 'inner', 0, 0, tiled=True)  2.17 us
  transfers between devices with their start and end apart: 6, of which 3 were waited for; matrix products, arithmetic and copies ran while one was open for 0% of the time, Pallas kernels for 39%

profile of v2, /device:TPU:0, one launch (start us, length us, event | category | flops | bytes accessed | tf_op | source)
XLA Modules:
  0.0 76.1 jit_solution(17333912671322452983)
XLA Ops:
  0.0 0.0 copy-start
  0.0 6.1 %shard_map.82 = (f32[512,256]{1,0:T(8,128)}, f32[256,256]{1,0:T(8,128)}, f32[4,512,128]{2,1,0:T(8,128)}) custom-call(f32[16,128]{1,0:T(8,128)} %bitcast.2, bf16[2048,512]{1,0:T(8,128)(2,1)} %y_hbm.5, bf16[2048,128]{1,0:T(8,128)(2,1)} %lu_hbm.5, bf16[2048,128]{1,0:T(8,128)(2,1)} %ll_hbm.5, bf16[2048,128]{1,0:T(8,128)(2,1)} %ru_hbm.3, bf16[2048,128]{1,0:T(8,128)(2,1)} %rl_hbm.3), custom_call_target="tpu_custom_call" | custom-call | flops 805306368 | bytes 1048576 | tf_op jit(solution)/shard_map/pallas_call | solution.py:26
  6.1 5.2 %all-to-all-start = ((f32[4,512,128]{2,1,0:T(8,128)}), f32[4,512,128]{2,1,0:T(8,128)S(1)}, u32[]{:S(2)}, u32[]{:S(2)}) async-start(f32[4,512,128]{2,1,0:T(8,128)} %get-tuple-element.20), calls=%async_computation | async-start | bytes 2097152 | tf_op jit(solution)/shard_map/all_to_all | solution.py:376
  11.3 0.0 copy-done
  11.3 11.5 %shard_map.83 = (bf16[2048,512]{1,0:T(8,128)(2,1)}, f32[16,72,128]{2,1,0:T(8,128)S(1)}, f32[640,128]{1,0:T(8,128)S(1)}, f32[128,256]{1,0:T(8,128)S(1)}) custom-call(s32[16,12]{1,0:T(8,128)S(1)} %copy-done, f32[16,128]{1,0:T(8,128)} %bitcast.3, bf16[16,12,128,128]{3,2,1,0:T(8,128)(2,1)} %blocks_hbm.5, bf16[2048,512]{1,0:T(8,128)(2,1)} %y_hbm.5, ...), custom_call_target="tpu_custom_call" | custom-call | flops 4294967296 | bytes 1048576 | tf_op jit(solution)/shard_map/pallas_call | solution.py:26
  22.8 2.2 %all-to-all-done.gathered_ref = f32[4,512,128]{2,1,0:T(8,128)S(1)} async-done(((f32[4,512,128]{2,1,0:T(8,128)}), f32[4,512,128]{2,1,0:T(8,128)S(1)}, u32[]{:S(2)}, u32[]{:S(2)}) %all-to-all-start) | async-done | bytes 1048608 | tf_op jit(solution)/shard_map/all_to_all | solution.py:376
  24.9 1.6 %shard_map.84 = (f32[16,72,128]{2,1,0:T(8,128)}, f32[640,128]{1,0:T(8,128)S(1)}, f32[512,128]{1,0:T(8,128)}) custom-call(s32[1]{0:T(128)} %bitcast.1.half_ref, f32[4,512,128]{2,1,0:T(8,128)S(1)} %all-to-all-done.gathered_ref, f32[16,72,128]{2,1,0:T(8,128)S(1)} %get-tuple-element.23.both_in_ref, f32[640,128]{1,0:T(8,128)S(1)} %get-tuple-element.24.low_in_ref, ...), custom_call_target="tpu_custom_call" | custom-call | flops 33554432 | bytes 1048576 | tf_op jit(solution)/shard_map/pallas_call | solution.py:26
  26.5 3.9 %all-to-all-start.1 = ((f32[16,72,128]{2,1,0:T(8,128)}), f32[16,72,128]{2,1,0:T(8,128)S(1)}, u32[]{:S(2)}, u32[]{:S(2)}) async-start(f32[16,72,128]{2,1,0:T(8,128)} %get-tuple-element.26), calls=%async_computation.1 | async-start | bytes 1179648 | tf_op jit(solution)/shard_map/all_to_all | solution.py:407
  30.5 2.0 %collective-permute-start.1 = (f32[640,128]{1,0:T(8,128)S(1)}, f32[640,128]{1,0:T(8,128)S(1)}, u32[]{:S(2)}, u32[]{:S(2)}) collective-permute-start(f32[640,128]{1,0:T(8,128)S(1)} %get-tuple-element.28), channel_id=1, source_target_pairs={{0,1},{1,0},{2,3},{3,2},{4,5},{5,4},{6,7},{7,6},{8,9},{9,8},{10,11... | collective-permute-start | bytes 983048 | tf_op jit(solution)/shard_map/ppermute | solution.py:333
  32.4 8.0 %shard_map.85.far_hbm = bf16[2048,256]{1,0:T(8,128)(2,1)} custom-call(s32[16,12]{1,0:T(8,128)S(1)} %copy-done, f32[16,128]{1,0:T(8,128)} %bitcast.4, bf16[16,12,128,128]{3,2,1,0:T(8,128)(2,1)} %blocks_hbm.5, bf16[2048,128]{1,0:T(8,128)(2,1)} %lu_hbm.5, bf16[2048,128]{1,0:T(8,128)(2,1)} %ll_hbm.5), custom_call_target="tpu_custom_call" | custom-call | flops 2147483648 | bytes 1048576 | tf_op jit(solution)/shard_map/pallas_call | solution.py:26
  40.5 0.0 all-to-all-done.1
  40.5 2.7 %collective-permute-start = (f32[72,128]{1,0:T(8,128)S(1)}, f32[72,128]{1,0:T(8,128)S(1)}, u32[]{:S(2)}, u32[]{:S(2)}) collective-permute-start(f32[72,128]{1,0:T(8,128)S(1)} %reduce_sum.9), channel_id=1, source_target_pairs={{0,16},{16,0},{1,17},{17,1},{2,18},{18,2},{3,19},{19,3},{4,20},{20... | collective-permute-start | bytes 110600 | tf_op jit(solution)/shard_map/ppermute | solution.py:333
  43.2 3.7 %collective-permute-done.1 = f32[640,128]{1,0:T(8,128)S(1)} collective-permute-done((f32[640,128]{1,0:T(8,128)S(1)}, f32[640,128]{1,0:T(8,128)S(1)}, u32[]{:S(2)}, u32[]{:S(2)}) %collective-permute-start.1) | collective-permute-done | bytes 327712 | tf_op jit(solution)/shard_map/ppermute | solution.py:333
  47.0 0.0 collective-permute-done
  47.0 1.0 %broadcast_in_dim.2 = f32[16,104,128]{2,1,0:T(8,128)} broadcast(f32[104,128]{1,0:T(8,128)S(1)} %pad_maximum_fusion), dimensions={1,2} | broadcast | bytes 905216 | tf_op jit(solution)/shard_map/broadcast_in_dim | solution.py:427
  48.0 3.7 %all-to-all-start.2 = ((f32[16,104,128]{2,1,0:T(8,128)}), f32[16,104,128]{2,1,0:T(8,128)S(1)}, u32[]{:S(2)}, u32[]{:S(2)}) async-start(f32[16,104,128]{2,1,0:T(8,128)} %broadcast_in_dim.2), calls=%async_computation.2 | async-start | bytes 1703936 | tf_op jit(solution)/shard_map/all_to_all | solution.py:428
  51.8 1.9 %collective-permute-start.2 = (f32[640,128]{1,0:T(8,128)S(1)}, f32[640,128]{1,0:T(8,128)S(1)}, u32[]{:S(2)}, u32[]{:S(2)}) collective-permute-start(f32[640,128]{1,0:T(8,128)S(1)} %add.4), channel_id=1, source_target_pairs={{0,2},{1,3},{2,0},{3,1},{4,6},{5,7},{6,4},{7,5},{8,10},{9,11},{10,... | collective-permute-start | bytes 983048 | tf_op jit(solution)/shard_map/ppermute | solution.py:333
  53.7 10.4 %shard_map.86.base_hbm = f32[2048,512]{1,0:T(8,128)} custom-call(s32[16,12]{1,0:T(8,128)S(1)} %copy-done, f32[16,128]{1,0:T(8,128)} %bitcast.5, bf16[16,12,128,128]{3,2,1,0:T(8,128)(2,1)} %blocks_hbm.5, bf16[2048,512]{1,0:T(8,128)(2,1)} %get-tuple-element.30.known_hbm, bf16[2048,512]{1,0:T(8,128)(2,1)} %y_hbm.5), custom_call_target="tpu_custom_call" | custom-call | flops 4294967296 | bytes 1048576 | tf_op jit(solution)/shard_map/pallas_call | solution.py:26
  64.1 6.9 %collective-permute-done.2.low_ref = f32[640,128]{1,0:T(8,128)S(1)} collective-permute-done((f32[640,128]{1,0:T(8,128)S(1)}, f32[640,128]{1,0:T(8,128)S(1)}, u32[]{:S(2)}, u32[]{:S(2)}) %collective-permute-start.2) | collective-permute-done | bytes 327712 | tf_op jit(solution)/shard_map/ppermute | solution.py:333
  71.0 0.0 all-to-all-done.2.upper_ref
  71.0 4.9 %shard_map.87 = f32[2048,512]{1,0:T(8,128)} custom-call(f32[16,128]{1,0:T(8,128)} %bitcast.6, f32[2048,512]{1,0:T(8,128)} %shard_map.86.base_hbm, bf16[2048,256]{1,0:T(8,128)(2,1)} %shard_map.85.far_hbm, bf16[2048,128]{1,0:T(8,128)(2,1)} %lu_hbm.5, bf16[2048,128]{1,0:T(8,128)(2,1)} %ll_hbm.5, f32[512,128]{1,0:T(8,128)} %get-tuple-element.32.sib_hbm, ...), custom_call_target="tpu_custom_call" | custom-call | flops 1073741824 | bytes 1048576 | tf_op jit(solution)/shard_map/pallas_call | solution.py:26
  (4 shorter events, 0.1 us)
Async XLA Ops:
  0.0 11.3 %copy-start = (s32[16,12]{1,0:T(8,128)S(1)}, s32[16,12]{1,0:T(8,128)}, u32[]{:S(2)}) copy-start(s32[16,12]{1,0:T(8,128)} %cols_ref.5) | copy-start | bytes 2308
  6.1 18.8 %all-to-all-start = ((f32[4,512,128]{2,1,0:T(8,128)}), f32[4,512,128]{2,1,0:T(8,128)S(1)}, u32[]{:S(2)}, u32[]{:S(2)}) async-start(f32[4,512,128]{2,1,0:T(8,128)} %get-tuple-element.20), calls=%async_computation | async-start | bytes 2097152 | tf_op jit(solution)/shard_map/all_to_all | solution.py:376
  26.5 14.0 %all-to-all-start.1 = ((f32[16,72,128]{2,1,0:T(8,128)}), f32[16,72,128]{2,1,0:T(8,128)S(1)}, u32[]{:S(2)}, u32[]{:S(2)}) async-start(f32[16,72,128]{2,1,0:T(8,128)} %get-tuple-element.26), calls=%async_computation.1 | async-start | bytes 1179648 | tf_op jit(solution)/shard_map/all_to_all | solution.py:407
  30.5 16.5 %collective-permute-start.1 = (f32[640,128]{1,0:T(8,128)S(1)}, f32[640,128]{1,0:T(8,128)S(1)}, u32[]{:S(2)}, u32[]{:S(2)}) collective-permute-start(f32[640,128]{1,0:T(8,128)S(1)} %get-tuple-element.28), channel_id=1, source_target_pairs={{0,1},{1,0},{2,3},{3,2},{4,5},{5,4},{6,7},{7,6},{8,9},{9,8},{10,11... | collective-permute-start | bytes 983048 | tf_op jit(solution)/shard_map/ppermute | solution.py:333
  40.5 6.4 %collective-permute-start = (f32[72,128]{1,0:T(8,128)S(1)}, f32[72,128]{1,0:T(8,128)S(1)}, u32[]{:S(2)}, u32[]{:S(2)}) collective-permute-start(f32[72,128]{1,0:T(8,128)S(1)} %reduce_sum.9), channel_id=1, source_target_pairs={{0,16},{16,0},{1,17},{17,1},{2,18},{18,2},{3,19},{19,3},{4,20},{20... | collective-permute-start | bytes 110600 | tf_op jit(solution)/shard_map/ppermute | solution.py:333
  48.0 23.0 %all-to-all-start.2 = ((f32[16,104,128]{2,1,0:T(8,128)}), f32[16,104,128]{2,1,0:T(8,128)S(1)}, u32[]{:S(2)}, u32[]{:S(2)}) async-start(f32[16,104,128]{2,1,0:T(8,128)} %broadcast_in_dim.2), calls=%async_computation.2 | async-start | bytes 1703936 | tf_op jit(solution)/shard_map/all_to_all | solution.py:428
  51.8 19.3 %collective-permute-start.2 = (f32[640,128]{1,0:T(8,128)S(1)}, f32[640,128]{1,0:T(8,128)S(1)}, u32[]{:S(2)}, u32[]{:S(2)}) collective-permute-start(f32[640,128]{1,0:T(8,128)S(1)} %add.4), channel_id=1, source_target_pairs={{0,2},{1,3},{2,0},{3,1},{4,6},{5,7},{6,4},{7,5},{8,10},{9,11},{10,... | collective-permute-start | bytes 983048 | tf_op jit(solution)/shard_map/ppermute | solution.py:333

commit v3 on v2

v3 whole, which is shorter than its diff:
```python
import functools

import jax
import jax.numpy as jnp
from jax import lax
from jax.experimental import pallas as pl
from jax.experimental.pallas import tpu as pltpu
from jax.sharding import Mesh
from jax.sharding import PartitionSpec as P

DAMPING = 0.9
F32 = jnp.float32
BF16 = jnp.bfloat16
VMEM = pl.BlockSpec(memory_space=pltpu.VMEM)
SMEM = pl.BlockSpec(memory_space=pltpu.SMEM)
FAR = pl.BlockSpec(memory_space=pltpu.HBM)


def shape(dims, dtype, near=False):
    return (pltpu.VMEM if near else pltpu.HBM)(dims, dtype)


def call(kernel, args, outs, scratch, megabytes, flops):
    values = [
        value if spec is SMEM else pltpu.with_memory_space_constraint(value, spec.memory_space)
        for value, spec in args
    ]
    return pl.pallas_call(
        kernel,
        out_shape=[out for out in outs],
        in_specs=[spec for _, spec in args],
        out_specs=[
            FAR if out.memory_space == pltpu.HBM else VMEM for out in outs
        ],
        scratch_shapes=scratch,
        cost_estimate=pl.CostEstimate(
            flops=flops, bytes_accessed=2**20, transcendentals=0
        ),
        compiler_params=pltpu.CompilerParams(vmem_limit_bytes=megabytes * 2**20),
    )(*values)


def dot(a, b):
    return jnp.dot(a, b, preferred_element_type=F32)


def tdot(a, b):
    return lax.dot_general(a, b, (((0,), (0,)), ((), ())), preferred_element_type=F32)


def start(source, target, sem):
    copy = pltpu.make_async_copy(source, target, sem)
    copy.start()
    return copy


def degree_columns(degree_ref):
    leaves, block = degree_ref.shape
    tall = jnp.concatenate([degree_ref[...]] * (block // leaves), axis=0)
    return tall.T[:, :leaves]


def scale_tile(columns, first, value):
    block = columns.shape[0]
    return jnp.concatenate(
        [
            columns[:, first + b : first + b + 1] * value[b * block : (b + 1) * block]
            for b in range(value.shape[0] // block)
        ],
        axis=0,
    )


def load_tiles(hbm, ref, tiles, sems, first):
    size = ref.shape[0] // tiles
    return [
        start(hbm.at[pl.ds(t * size, size)], ref.at[pl.ds(t * size, size)], sems.at[first + t])
        for t in range(tiles)
    ]


def first_kernel(
    degree_hbm, y_hbm, rl_hbm,
    lower_ref,
    degree_ref, y_ref, right_ref, scaled_ref, sems,
):
    block = degree_ref.shape[1]
    tiles = 4
    size = y_ref.shape[0] // tiles
    degree_copy = start(degree_hbm, degree_ref, sems.at[tiles])
    right_copy = start(rl_hbm, right_ref, sems.at[tiles + 1])
    loads = load_tiles(y_hbm, y_ref, tiles, sems, 0)
    degree_copy.wait()
    columns = degree_columns(degree_ref)
    right_copy.wait()
    for tile in range(tiles):
        loads[tile].wait()
        rows = slice(tile * size, (tile + 1) * size)
        value = y_ref[rows, :].astype(F32)
        scaled_ref[rows, :] = scale_tile(columns, tile * size // block, value).astype(BF16)
    lower_ref[...] = tdot(scaled_ref[...], right_ref[...])


def place(cols_ref, blocks_ref, dense_ref):
    leaves, stored, block, _ = blocks_ref.shape
    for row in range(leaves):
        rows = slice(row * block, (row + 1) * block)
        dense_ref[rows, :] = jnp.zeros((block, leaves * block), BF16)
        for j in range(stored):
            col = pl.multiple_of(cols_ref[row, j] * block, block)
            dense_ref[rows, pl.ds(col, block)] = blocks_ref[row, j]


def known_kernel(
    cols_hbm, degree_hbm, blocks_hbm, y_hbm, lu_hbm, ll_hbm, ru_hbm, rl_hbm,
    known_hbm, dense_hbm, both_ref, low_ref, lower_coupling_ref,
    cols_ref, degree_ref, blocks_ref, dense_ref, y_ref, scaled_ref, known_ref, left_ref, spread_ref, right_ref, sems,
):
    leaves, _, block, _ = blocks_ref.shape
    rank = ru_hbm.shape[1]
    sides = [
        start(a, b, sems.at[i])
        for i, (a, b) in enumerate(
            (
                (degree_hbm, degree_ref),
                (cols_hbm, cols_ref),
                (lu_hbm, left_ref.at[:, pl.ds(0, rank)]),
                (ll_hbm, left_ref.at[:, pl.ds(rank, rank)]),
                (ru_hbm, right_ref.at[:, pl.ds(0, rank)]),
                (rl_hbm, right_ref.at[:, pl.ds(rank, rank)]),
                (y_hbm, y_ref),
            )
        )
    ]
    sides[0].wait()
    columns = degree_columns(degree_ref)
    square = columns * columns
    loads = load_tiles(blocks_hbm, blocks_ref, 4, sems, 7)
    for side in sides[1:]:
        side.wait()
    for leaf in range(leaves):
        rows = slice(leaf * block, (leaf + 1) * block)
        spread_ref[rows, :] = scale_tile(square, leaf, left_ref[rows, :].astype(F32)).astype(BF16)
        scaled_ref[rows, :] = scale_tile(columns, leaf, y_ref[rows, :].astype(F32)).astype(BF16)
    coupling = tdot(spread_ref[...], right_ref[...])
    parts, height, _ = both_ref.shape
    cols = scaled_ref.shape[1]
    width = cols // parts
    lines = rank // parts
    both_ref[:, :width, :] = tdot(scaled_ref[...], right_ref[:, :rank]).reshape(parts, width, rank)
    both_ref[:, 2 * width :, :] = coupling[:rank, :rank].reshape(parts, lines, rank)
    low_ref[cols:, :] = coupling[:rank, rank:]
    lower_coupling_ref[...] = coupling[rank:, :]
    for load in loads:
        load.wait()
    place(cols_ref, blocks_ref, dense_ref)
    outs = [start(dense_ref, dense_hbm, sems.at[0])]
    tiles = 4
    size = y_ref.shape[0] // tiles
    for tile in range(tiles):
        rows = slice(tile * size, (tile + 1) * size)
        first = tile * size // block
        product = dot(dense_ref[rows, :], scaled_ref[...])
        value = y_ref[rows, :].astype(F32) + DAMPING * scale_tile(columns, first, product)
        known_ref[rows, :] = scale_tile(columns, first, value).astype(BF16)
    outs.append(start(known_ref, known_hbm, sems.at[1]))
    found = tdot(known_ref[...], right_ref[...])
    low_ref[:cols, :] = found[:, rank:]
    both_ref[:, width : 2 * width, :] = found[:, :rank].reshape(parts, width, rank)
    for out in outs:
        out.wait()


def pack_kernel(*refs):
    both_in_ref, low_in_ref, coupling_ref = refs[:3]
    received = refs[3:-6]
    both_ref, low_a_ref, low_b_ref, sib_hbm, sib_ref, sem = refs[-6:]
    sib = received[0][...]
    for other in received[1:]:
        sib = sib + other[...]
    sib_ref[...] = sib
    out = start(sib_ref, sib_hbm, sem)
    cols, rank = sib.shape
    update = dot((DAMPING * sib).astype(BF16), coupling_ref[...].astype(BF16))
    parts, height, _ = both_ref.shape
    width = cols // parts
    both_ref[:, :width, :] = both_in_ref[:, :width, :]
    both_ref[:, 2 * width :, :] = both_in_ref[:, 2 * width :, :]
    both_ref[:, width : 2 * width, :] = both_in_ref[:, width : 2 * width, :] + update[
        :, :rank
    ].reshape(parts, width, rank)
    half = low_a_ref.shape[0]
    low_a_ref[...] = low_in_ref[:half, :] + update[:half, rank:]
    low_b_ref[: cols - half, :] = low_in_ref[half:cols, :] + update[half:, rank:]
    low_b_ref[cols - half :, :] = low_in_ref[cols:, :]
    out.wait()


def far_kernel(
    degree_hbm, dense_hbm, lu_hbm, ll_hbm,
    far_hbm,
    degree_ref, dense_ref, left_ref, spread_ref, far_ref, sems,
):
    leaves, block = degree_ref.shape
    rank = lu_hbm.shape[1]
    tiles = 4
    sides = [
        start(degree_hbm, degree_ref, sems.at[tiles]),
        start(lu_hbm, left_ref.at[:, pl.ds(0, rank)], sems.at[tiles + 1]),
        start(ll_hbm, left_ref.at[:, pl.ds(rank, rank)], sems.at[tiles + 2]),
    ]
    copies = load_tiles(dense_hbm, dense_ref, tiles, sems, 0)
    for side in sides:
        side.wait()
    columns = degree_columns(degree_ref)
    square = columns * columns
    for leaf in range(leaves):
        rows = slice(leaf * block, (leaf + 1) * block)
        spread_ref[rows, :] = scale_tile(square, leaf, left_ref[rows, :].astype(F32)).astype(BF16)
    for copy in copies:
        copy.wait()
    far_ref[...] = (DAMPING * dot(dense_ref[...], spread_ref[...])).astype(BF16)
    start(far_ref, far_hbm, sems.at[0]).wait()


def local_kernel(
    dense_hbm, known_hbm,
    local_hbm,
    dense_ref, known_ref, local_ref, sems,
):
    tiles = 4
    size = dense_ref.shape[0] // tiles
    known_copy = start(known_hbm, known_ref, sems.at[tiles])
    loads = load_tiles(dense_hbm, dense_ref, tiles, sems, 0)
    known_copy.wait()
    for load in loads:
        load.wait()
    outs = []
    for half in range(2):
        rows = slice(half * 2 * size, (half + 1) * 2 * size)
        near = pl.ds(half * 2 * size, 2 * size)
        local_ref[rows, :] = (DAMPING * dot(dense_ref[rows, :], known_ref[...])).astype(BF16)
        outs.append(start(local_ref.at[near], local_hbm.at[near], sems.at[half]))
    for out in outs:
        out.wait()


def final_kernel(
    inner, core_ref, degree_hbm, far_hbm, lu_hbm, ll_hbm, sib_hbm, y_hbm, local_hbm, mine_ref, other_ref, low_a_ref, low_b_ref,
    out_hbm,
    degree_ref, left_ref, coef_ref, sib_ref, own_ref, first_ref, second_ref, across_ref, low_ref, y_ref, local_ref, stage_ref, sems,
):
    tiles = 4
    rank = lu_hbm.shape[1]
    block = degree_ref.shape[1]
    size = stage_ref.shape[0] // tiles
    degree_copy = start(degree_hbm, degree_ref, sems.at[0])
    sib_copy = start(sib_hbm, sib_ref, sems.at[1])
    sides = [
        start(far_hbm, left_ref.at[:, pl.ds(0, 2 * rank)], sems.at[2]),
        start(lu_hbm, left_ref.at[:, pl.ds(2 * rank, rank)], sems.at[3]),
        start(ll_hbm, left_ref.at[:, pl.ds(3 * rank, rank)], sems.at[4]),
    ]
    loads = load_tiles(y_hbm, y_ref, tiles, sems, 5)
    others = load_tiles(local_hbm, local_ref, tiles, sems, 9)
    slots = mine_ref.shape[0]
    cols = own_ref.shape[0]
    width = cols // (2 * slots)
    lines = rank // (2 * slots)
    for source, core in ((mine_ref, core_ref[0]), (other_ref, 1 - core_ref[0])):
        for rest in range(slots // inner):
            some = source[rest * inner : (rest + 1) * inner]
            span = inner * width
            at = pl.ds(pl.multiple_of((2 * rest + core) * span, span), span)
            own_ref[at, :] = some[:, :width].reshape(span, rank)
            first_ref[at, :] = some[:, width : 2 * width].reshape(span, rank)
            second_ref[at, :] = some[:, 2 * width : 3 * width].reshape(span, rank)
            span = inner * lines
            at = pl.ds(pl.multiple_of((2 * rest + core) * span, span), span)
            across_ref[at, :] = some[:, 3 * width :].reshape(span, rank)
    half = low_a_ref.shape[0]
    low_ref[:half, :] = low_a_ref[...]
    low_ref[half:, :] = low_b_ref[...]
    first = first_ref[...]
    second = second_ref[...] + dot(
        own_ref[...].astype(BF16), (DAMPING * across_ref[...]).astype(BF16)
    )
    down = (DAMPING * low_ref[cols:, :]).astype(BF16)
    lower = low_ref[:cols, :] + dot(first.astype(BF16), down)
    sib_copy.wait()
    coef_ref[:, 0 * rank : 1 * rank] = (DAMPING * first).astype(BF16)
    coef_ref[:, 1 * rank : 2 * rank] = (DAMPING * sib_ref[...]).astype(BF16)
    coef_ref[:, 2 * rank : 3 * rank] = (DAMPING * second).astype(BF16)
    coef_ref[:, 3 * rank : 4 * rank] = (DAMPING * lower).astype(BF16)
    degree_copy.wait()
    columns = degree_columns(degree_ref)
    for side in sides:
        side.wait()
    outs = []
    for tile in range(tiles):
        rows = slice(tile * size, (tile + 1) * size)
        near = pl.ds(tile * size, size)
        product = lax.dot_general(
            left_ref[rows, :], coef_ref[...], (((1,), (1,)), ((), ())), preferred_element_type=F32
        )
        loads[tile].wait()
        others[tile].wait()
        stage_ref[rows, :] = y_ref[rows, :].astype(F32) + scale_tile(
            columns, tile * size // block, local_ref[rows, :].astype(F32) + product
        )
        outs.append(start(stage_ref.at[near], out_hbm.at[near], sems.at[tile]))
    for out in outs:
        out.wait()


def partner(value, axis, mask):
    pairs = [(source, source ^ mask) for source in range(lax.axis_size(axis))]
    return lax.ppermute(value, axis, pairs)


def low_bits(axis):
    masks = []
    while 2 ** (len(masks) + 1) < lax.axis_size(axis):
        masks.append(2 ** len(masks))
    return masks


def body(
    queries,
    inv_sqrt_degree,
    leaf_blocks,
    block_cols,
    left_upper,
    right_upper,
    left_lower,
    right_lower,
):
    inner = lax.axis_size("inner")
    parts = inner * lax.axis_size("rest") * lax.axis_size("core")
    rows, cols = queries.shape
    rank = left_upper.shape[1]
    leaves, stored, block, _ = leaf_blocks.shape
    degree = inv_sqrt_degree.reshape(leaves, block)
    width, lines = cols // parts, rank // parts
    height = 2 * width + lines
    node = ("rest", "core", "inner")
    dma = pltpu.SemaphoreType.DMA
    degree_scratch = pltpu.VMEM((leaves, block), F32)

    def scratch(*dims):
        return pltpu.VMEM(dims, BF16)

    def wide(*dims):
        return pltpu.VMEM(dims, F32)

    (first_lower,) = call(
        first_kernel,
        [(degree, FAR), (queries, FAR), (right_lower, FAR)],
        [shape((cols, rank), F32, True)],
        [degree_scratch, scratch(rows, cols), scratch(rows, rank), scratch(rows, cols), dma((6,))],
        8,
        2 * rows * cols * rank,
    )
    first_sib = [
        partner(first_lower, "inner", inner // 2 + other) for other in range(inner // 2)
    ]

    known, dense, both, low, lower_coupling = call(
        known_kernel,
        [(block_cols, FAR), (degree, FAR), (leaf_blocks, FAR), (queries, FAR)]
        + [(left_upper, FAR), (left_lower, FAR), (right_upper, FAR), (right_lower, FAR)],
        [
            shape((rows, cols), BF16),
            shape((rows, rows), BF16),
            shape((parts, height, rank), F32, True),
            shape((cols + rank, rank), F32, True),
            shape((rank, 2 * rank), F32, True),
        ],
        [pltpu.SMEM((leaves, stored), jnp.int32), degree_scratch]
        + [scratch(leaves, stored, block, block), scratch(rows, rows)]
        + [scratch(rows, cols)] * 3
        + [scratch(rows, 2 * rank)] * 3
        + [dma((11,))],
        36,
        2 * rows * rows * cols,
    )
    split = (cols + rank) // 2
    both, low_a, low_b, sib_lower = call(
        pack_kernel,
        [(both, VMEM), (low, VMEM), (lower_coupling, VMEM)] + [(value, VMEM) for value in first_sib],
        [
            shape((parts, height, rank), F32, True),
            shape((split, rank), F32, True),
            shape((cols + rank - split, rank), F32, True),
            shape((cols, rank), F32),
        ],
        [wide(cols, rank), dma(())],
        8,
        4 * cols * rank * rank,
    )
    both = lax.all_to_all(both, node, 0, 0, tiled=True)

    (far,) = call(
        far_kernel,
        [(degree, FAR), (dense, FAR), (left_upper, FAR), (left_lower, FAR)],
        [shape((rows, 2 * rank), BF16)],
        [degree_scratch, scratch(rows, rows)] + [scratch(rows, 2 * rank)] * 3 + [dma((7,))],
        20,
        4 * rows * rows * rank,
    )
    both, far = lax.optimization_barrier((both, far))
    both = both.sum(axis=0)
    received = partner(both, "node", 1)

    for mask in low_bits("inner"):
        low_a = low_a + partner(low_a, "inner", mask)
    low_b = partner(low_b, "inner", inner // 2)

    received, low_a, low_b, known = lax.optimization_barrier((received, low_a, low_b, known))
    sib = jnp.concatenate([both[:width], received], axis=0)
    sib = jnp.broadcast_to(sib[None], (parts // 2,) + sib.shape)
    sib = lax.all_to_all(sib, ("rest", "inner"), 0, 0, tiled=True)
    low_a = partner(low_a, "inner", inner // 2)
    for mask in low_bits("inner"):
        low_b = low_b + partner(low_b, "inner", mask)

    (local,) = call(
        local_kernel,
        [(dense, FAR), (known, FAR)],
        [shape((rows, cols), BF16)],
        [scratch(rows, rows), scratch(rows, cols), scratch(rows, cols), dma((5,))],
        20,
        2 * rows * rows * cols,
    )

    sib, local, low_a, low_b = lax.optimization_barrier((sib, local, low_a, low_b))
    other = partner(sib, "core", 1)
    core = lax.axis_index("core").astype(jnp.int32).reshape(1)
    (out,) = call(
        functools.partial(final_kernel, inner),
        [(core, SMEM), (degree, FAR), (far, FAR), (left_upper, FAR), (left_lower, FAR), (sib_lower, FAR)]
        + [(queries, FAR), (local, FAR), (sib, VMEM), (other, VMEM), (low_a, VMEM), (low_b, VMEM)],
        [shape((rows, cols), F32)],
        [degree_scratch, scratch(rows, 4 * rank), scratch(cols, 4 * rank)]
        + [wide(cols, rank)] * 4
        + [wide(rank, rank), wide(cols + rank, rank), scratch(rows, cols), scratch(rows, cols)]
        + [wide(rows, cols), dma((13,))],
        20,
        8 * rows * cols * rank,
    )
    return out


def solution(mesh):
    outer, inner = mesh.devices.shape
    fine = Mesh(mesh.devices.reshape(2, outer // 4, 2, inner), ("node", "rest", "core", "inner"))
    rows = P(("node", "rest", "core", "inner"))
    return jax.shard_map(
        body, mesh=fine, in_specs=(rows,) * 8, out_specs=rows, check_vma=False
    )
```

time: 76.4 us -> 65.8 us (0.86)
  waiting for transfers between devices: 12.8 us -> 3.99 us
  Pallas kernels: 42.5 us -> 38.7 us
  starting transfers between devices: 19.4 us -> 21.5 us
    ppermute x3 -> x8, starting transfers between devices: 6.56 us -> 14 us  [partner(): return lax.ppermute(value, axis, pairs)]
    ppermute x3 -> x8, waiting for transfers between devices: 10.6 us -> 3.99 us  [partner(): return lax.ppermute(value, axis, pairs)]
    all_to_all x3 -> x2, starting transfers between devices: 12.9 us -> 7.55 us  [the longest x1 3.91 us: body(): both = lax.all_to_all(both, node, 0, 0, tiled=True)]
    pallas_call x6, Pallas kernels: 42.5 us -> 38.7 us  [call(): pl.pallas_call(kernel, out_shape=[out for out in outs], in_specs=[spec fo...]
    all_to_all x3 -> x2, waiting for transfers between devices: 2.17 us -> 0.01 us  [the longest x1 0.01 us: body(): both = lax.all_to_all(both, node, 0, 0, tiled=True)]
  transfers between devices with their start and end apart: 6 -> 10, of which waited for: 3 -> 2; matrix products, arithmetic and copies ran while one was open for 0% -> 0% of each run, Pallas kernels for 39% -> 45%
where the time goes in v3:
time: 65.8 us; the launch traced here: 65.4 us
  Pallas kernels  38.7 us (59%)
  starting transfers between devices  21.5 us (33%)
  waiting for transfers between devices  3.99 us (6%)
  local copies, waits for them, and re-layouts  0.78 us (1%)
    pallas_call x6, Pallas kernels, call(): pl.pallas_call(kernel, out_shape=[out for out in outs], in_specs=[spec fo...  38.7 us
    ppermute x8, starting transfers between devices, partner(): return lax.ppermute(value, axis, pairs)  14 us
    ppermute x8, waiting for transfers between devices, partner(): return lax.ppermute(value, axis, pairs)  3.99 us
    all_to_all x1, starting transfers between devices, body(): both = lax.all_to_all(both, node, 0, 0, tiled=True)  3.91 us
    all_to_all x1, starting transfers between devices, body(): sib = lax.all_to_all(sib, ('rest', 'inner'), 0, 0, tiled=True)  3.64 us
  transfers between devices with their start and end apart: 10, of which 2 were waited for; matrix products, arithmetic and copies ran while one was open for 0% of the time, Pallas kernels for 45%

profile of v3, /device:TPU:0, one launch (start us, length us, event | category | flops | bytes accessed | tf_op | source)
XLA Modules:
  0.0 65.4 jit_solution(15044699211372277643)
XLA Ops:
  0.0 2.6 %shard_map.83 = f32[512,128]{1,0:T(8,128)S(1)} custom-call(f32[16,128]{1,0:T(8,128)} %bitcast.2, bf16[2048,512]{1,0:T(8,128)(2,1)} %y_hbm.5, bf16[2048,128]{1,0:T(8,128)(2,1)} %rl_hbm.3), custom_call_target="tpu_custom_call" | custom-call | flops 268435456 | bytes 1048576 | tf_op jit(solution)/shard_map/pallas_call | solution.py:28
  2.6 4.0 %collective-permute-start.1 = (f32[512,128]{1,0:T(8,128)S(1)}, f32[512,128]{1,0:T(8,128)S(1)}, u32[]{:S(2)}, u32[]{:S(2)}) collective-permute-start(f32[512,128]{1,0:T(8,128)S(1)} %shard_map.83), channel_id=1, source_target_pairs={{0,3},{1,2},{2,1},{3,0},{4,7},{5,6},{6,5},{7,4},{8,11},{9,10},{10,... | collective-permute-start | bytes 786440 | tf_op jit(solution)/shard_map/ppermute | solution.py:318
  6.6 0.5 collective-permute-start
  7.1 12.4 %shard_map.82 = (bf16[2048,512]{1,0:T(8,128)(2,1)}, bf16[2048,2048]{1,0:T(8,128)(2,1)}, f32[16,72,128]{2,1,0:T(8,128)S(1)}, f32[640,128]{1,0:T(8,128)S(1)}, f32[128,256]{1,0:T(8,128)S(1)}) custom-call(s32[16,12]{1,0:T(8,128)} %cols_hbm.1, f32[16,128]{1,0:T(8,128)} %bitcast.3, bf16[16,12,128,128]{3,2,1,0:T(8,128)(2,1)} %blocks_hbm.1, ...), custom_call_target="tpu_custom_call" | custom-call | flops 4294967296 | bytes 1048576 | tf_op jit(solution)/shard_map/pallas_call | solution.py:28
  19.5 0.0 collective-permute-done.1.refs_4_
  19.5 0.0 collective-permute-done.refs_3_
  19.6 1.6 %shard_map.84 = (f32[16,72,128]{2,1,0:T(8,128)}, f32[320,128]{1,0:T(8,128)S(1)}, f32[320,128]{1,0:T(8,128)S(1)}, f32[512,128]{1,0:T(8,128)}) custom-call(f32[16,72,128]{2,1,0:T(8,128)S(1)} %get-tuple-element.24.refs_0_, f32[640,128]{1,0:T(8,128)S(1)} %get-tuple-element.25.refs_1_, f32[128,256]{1,0:T(8,128)S(1)} %get-tuple-element.26.refs_2_, ...), custom_call_target="tpu_custom_call" | custom-call | flops 33554432 | bytes 1048576 | tf_op jit(solution)/shard_map/pallas_call | solution.py:28
  21.2 3.9 %all-to-all-start = ((f32[16,72,128]{2,1,0:T(8,128)}), f32[16,72,128]{2,1,0:T(8,128)S(1)}, u32[]{:S(2)}, u32[]{:S(2)}) async-start(f32[16,72,128]{2,1,0:T(8,128)} %get-tuple-element.27), calls=%async_computation | async-start | bytes 1179648 | tf_op jit(solution)/shard_map/all_to_all | solution.py:401
  25.1 1.9 %collective-permute-start.4 = (f32[320,128]{1,0:T(8,128)S(1)}, f32[320,128]{1,0:T(8,128)S(1)}, u32[]{:S(2)}, u32[]{:S(2)}) collective-permute-start(f32[320,128]{1,0:T(8,128)S(1)} %get-tuple-element.33), channel_id=1, source_target_pairs={{0,2},{1,3},{2,0},{3,1},{4,6},{5,7},{6,4},{7,5},{8,10},{9,11},{10,... | collective-permute-start | bytes 491528 | tf_op jit(solution)/shard_map/ppermute | solution.py:318
  27.0 1.5 %collective-permute-start.3 = (f32[320,128]{1,0:T(8,128)S(1)}, f32[320,128]{1,0:T(8,128)S(1)}, u32[]{:S(2)}, u32[]{:S(2)}) collective-permute-start(f32[320,128]{1,0:T(8,128)S(1)} %get-tuple-element.32), channel_id=1, source_target_pairs={{0,1},{1,0},{2,3},{3,2},{4,5},{5,4},{6,7},{7,6},{8,9},{9,8},{10,11... | collective-permute-start | bytes 491528 | tf_op jit(solution)/shard_map/ppermute | solution.py:318
  28.5 7.2 %shard_map.85.far_hbm = bf16[2048,256]{1,0:T(8,128)(2,1)} custom-call(f32[16,128]{1,0:T(8,128)} %bitcast.4, bf16[2048,2048]{1,0:T(8,128)(2,1)} %get-tuple-element.28.dense_hbm, bf16[2048,128]{1,0:T(8,128)(2,1)} %lu_hbm.5, bf16[2048,128]{1,0:T(8,128)(2,1)} %ll_hbm.5), custom_call_target="tpu_custom_call" | custom-call | flops 2147483648 | bytes 1048576 | tf_op jit(solution)/shard_map/pallas_call | solution.py:28
  35.7 0.0 all-to-all-done
  35.7 2.7 %collective-permute-start.2 = (f32[72,128]{1,0:T(8,128)S(1)}, f32[72,128]{1,0:T(8,128)S(1)}, u32[]{:S(2)}, u32[]{:S(2)}) collective-permute-start(f32[72,128]{1,0:T(8,128)S(1)} %reduce_sum.9), channel_id=1, source_target_pairs={{0,16},{16,0},{1,17},{17,1},{2,18},{18,2},{3,19},{19,3},{4,20},{20... | collective-permute-start | bytes 110600 | tf_op jit(solution)/shard_map/ppermute | solution.py:318
  38.4 0.0 collective-permute-done.3
  38.4 0.0 collective-permute-done.4
  38.4 2.2 %collective-permute-done.2 = f32[72,128]{1,0:T(8,128)S(1)} collective-permute-done((f32[72,128]{1,0:T(8,128)S(1)}, f32[72,128]{1,0:T(8,128)S(1)}, u32[]{:S(2)}, u32[]{:S(2)}) %collective-permute-start.2) | collective-permute-done | bytes 36896 | tf_op jit(solution)/shard_map/ppermute | solution.py:318
  40.7 0.8 %broadcast_in_dim.2 = f32[8,104,128]{2,1,0:T(8,128)} broadcast(f32[104,128]{1,0:T(8,128)S(1)} %pad_maximum_fusion), dimensions={1,2} | broadcast | bytes 479232 | tf_op jit(solution)/shard_map/broadcast_in_dim | solution.py:421
  41.4 3.6 %all-to-all-start.1 = ((f32[8,104,128]{2,1,0:T(8,128)}), f32[8,104,128]{2,1,0:T(8,128)S(1)}, u32[]{:S(2)}, u32[]{:S(2)}) async-start(f32[8,104,128]{2,1,0:T(8,128)} %broadcast_in_dim.2), calls=%async_computation.1 | async-start | bytes 851968 | tf_op jit(solution)/shard_map/all_to_all | solution.py:422
  45.1 1.9 %collective-permute-start.5 = (f32[320,128]{1,0:T(8,128)S(1)}, f32[320,128]{1,0:T(8,128)S(1)}, u32[]{:S(2)}, u32[]{:S(2)}) collective-permute-start(f32[320,128]{1,0:T(8,128)S(1)} %add.6), channel_id=1, source_target_pairs={{0,2},{1,3},{2,0},{3,1},{4,6},{5,7},{6,4},{7,5},{8,10},{9,11},{10,... | collective-permute-start | bytes 491528 | tf_op jit(solution)/shard_map/ppermute | solution.py:318
  47.0 1.5 %collective-permute-start.6 = (f32[320,128]{1,0:T(8,128)S(1)}, f32[320,128]{1,0:T(8,128)S(1)}, u32[]{:S(2)}, u32[]{:S(2)}) collective-permute-start(f32[320,128]{1,0:T(8,128)S(1)} %collective-permute-done.4), channel_id=1, source_target_pairs={{0,1},{1,0},{2,3},{3,2},{4,5},{5,4},{6,7},{7,6},{8,9},{9,8},{10,11... | collective-permute-start | bytes 491528 | tf_op jit(solution)/shard_map/ppermute | solution.py:318
  48.5 9.5 %shard_map.86.local_hbm = bf16[2048,512]{1,0:T(8,128)(2,1)} custom-call(bf16[2048,2048]{1,0:T(8,128)(2,1)} %get-tuple-element.28.dense_hbm, bf16[2048,512]{1,0:T(8,128)(2,1)} %get-tuple-element.36.known_hbm), custom_call_target="tpu_custom_call" | custom-call | flops 4294967296 | bytes 1048576 | tf_op jit(solution)/shard_map/pallas_call | solution.py:28
  58.0 0.0 collective-permute-done.6
  58.1 0.0 collective-permute-done.5.low_a_ref
  58.1 0.0 all-to-all-done.1.mine_ref
  58.1 0.1 collective-permute-start.7
  58.2 1.8 %collective-permute-done.7.other_ref = f32[8,104,128]{2,1,0:T(8,128)S(1)} collective-permute-done((f32[8,104,128]{2,1,0:T(8,128)S(1)}, f32[8,104,128]{2,1,0:T(8,128)S(1)}, u32[]{:S(2)}, u32[]{:S(2)}) %collective-permute-start.7) | collective-permute-done | bytes 426016 | tf_op jit(solution)/shard_map/ppermute | solution.py:318
  59.9 5.3 %shard_map.87 = f32[2048,512]{1,0:T(8,128)} custom-call(s32[1]{0:T(128)} %bitcast.core_ref, f32[16,128]{1,0:T(8,128)} %bitcast.5, bf16[2048,256]{1,0:T(8,128)(2,1)} %shard_map.85.far_hbm, bf16[2048,128]{1,0:T(8,128)(2,1)} %lu_hbm.5, bf16[2048,128]{1,0:T(8,128)(2,1)} %ll_hbm.5, f32[512,128]{1,0:T(8,128)} %get-tuple-element.30.sib_hbm, ...), custom_call_target="tpu_custom_call" | custom-call | flops 1073741824 | bytes 1048576 | tf_op jit(solution)/shard_map/pallas_call | solution.py:28
  (5 shorter events, 0.1 us)
Async XLA Ops:
  2.6 16.9 %collective-permute-start.1 = (f32[512,128]{1,0:T(8,128)S(1)}, f32[512,128]{1,0:T(8,128)S(1)}, u32[]{:S(2)}, u32[]{:S(2)}) collective-permute-start(f32[512,128]{1,0:T(8,128)S(1)} %shard_map.83), channel_id=1, source_target_pairs={{0,3},{1,2},{2,1},{3,0},{4,7},{5,6},{6,5},{7,4},{8,11},{9,10},{10,... | collective-permute-start | bytes 786440 | tf_op jit(solution)/shard_map/ppermute | solution.py:318
  6.6 13.0 %collective-permute-start = (f32[512,128]{1,0:T(8,128)S(1)}, f32[512,128]{1,0:T(8,128)S(1)}, u32[]{:S(2)}, u32[]{:S(2)}) collective-permute-start(f32[512,128]{1,0:T(8,128)S(1)} %shard_map.83), channel_id=1, source_target_pairs={{0,2},{1,3},{2,0},{3,1},{4,6},{5,7},{6,4},{7,5},{8,10},{9,11},{10,... | collective-permute-start | bytes 786440 | tf_op jit(solution)/shard_map/ppermute | solution.py:318
  21.2 14.5 %all-to-all-start = ((f32[16,72,128]{2,1,0:T(8,128)}), f32[16,72,128]{2,1,0:T(8,128)S(1)}, u32[]{:S(2)}, u32[]{:S(2)}) async-start(f32[16,72,128]{2,1,0:T(8,128)} %get-tuple-element.27), calls=%async_computation | async-start | bytes 1179648 | tf_op jit(solution)/shard_map/all_to_all | solution.py:401
  25.1 13.3 %collective-permute-start.4 = (f32[320,128]{1,0:T(8,128)S(1)}, f32[320,128]{1,0:T(8,128)S(1)}, u32[]{:S(2)}, u32[]{:S(2)}) collective-permute-start(f32[320,128]{1,0:T(8,128)S(1)} %get-tuple-element.33), channel_id=1, source_target_pairs={{0,2},{1,3},{2,0},{3,1},{4,6},{5,7},{6,4},{7,5},{8,10},{9,11},{10,... | collective-permute-start | bytes 491528 | tf_op jit(solution)/shard_map/ppermute | solution.py:318
  27.0 11.4 %collective-permute-start.3 = (f32[320,128]{1,0:T(8,128)S(1)}, f32[320,128]{1,0:T(8,128)S(1)}, u32[]{:S(2)}, u32[]{:S(2)}) collective-permute-start(f32[320,128]{1,0:T(8,128)S(1)} %get-tuple-element.32), channel_id=1, source_target_pairs={{0,1},{1,0},{2,3},{3,2},{4,5},{5,4},{6,7},{7,6},{8,9},{9,8},{10,11... | collective-permute-start | bytes 491528 | tf_op jit(solution)/shard_map/ppermute | solution.py:318
  35.7 4.9 %collective-permute-start.2 = (f32[72,128]{1,0:T(8,128)S(1)}, f32[72,128]{1,0:T(8,128)S(1)}, u32[]{:S(2)}, u32[]{:S(2)}) collective-permute-start(f32[72,128]{1,0:T(8,128)S(1)} %reduce_sum.9), channel_id=1, source_target_pairs={{0,16},{16,0},{1,17},{17,1},{2,18},{18,2},{3,19},{19,3},{4,20},{20... | collective-permute-start | bytes 110600 | tf_op jit(solution)/shard_map/ppermute | solution.py:318
  41.4 16.6 %all-to-all-start.1 = ((f32[8,104,128]{2,1,0:T(8,128)}), f32[8,104,128]{2,1,0:T(8,128)S(1)}, u32[]{:S(2)}, u32[]{:S(2)}) async-start(f32[8,104,128]{2,1,0:T(8,128)} %broadcast_in_dim.2), calls=%async_computation.1 | async-start | bytes 851968 | tf_op jit(solution)/shard_map/all_to_all | solution.py:422
  45.1 13.0 %collective-permute-start.5 = (f32[320,128]{1,0:T(8,128)S(1)}, f32[320,128]{1,0:T(8,128)S(1)}, u32[]{:S(2)}, u32[]{:S(2)}) collective-permute-start(f32[320,128]{1,0:T(8,128)S(1)} %add.6), channel_id=1, source_target_pairs={{0,2},{1,3},{2,0},{3,1},{4,6},{5,7},{6,4},{7,5},{8,10},{9,11},{10,... | collective-permute-start | bytes 491528 | tf_op jit(solution)/shard_map/ppermute | solution.py:318
  47.0 11.0 %collective-permute-start.6 = (f32[320,128]{1,0:T(8,128)S(1)}, f32[320,128]{1,0:T(8,128)S(1)}, u32[]{:S(2)}, u32[]{:S(2)}) collective-permute-start(f32[320,128]{1,0:T(8,128)S(1)} %collective-permute-done.4), channel_id=1, source_target_pairs={{0,1},{1,0},{2,3},{3,2},{4,5},{5,4},{6,7},{7,6},{8,9},{9,8},{10,11... | collective-permute-start | bytes 491528 | tf_op jit(solution)/shard_map/ppermute | solution.py:318
  58.1 1.8 %collective-permute-start.7 = (f32[8,104,128]{2,1,0:T(8,128)S(1)}, f32[8,104,128]{2,1,0:T(8,128)S(1)}, u32[]{:S(2)}, u32[]{:S(2)}) collective-permute-start(f32[8,104,128]{2,1,0:T(8,128)S(1)} %all-to-all-done.1.mine_ref), channel_id=1, source_target_pairs={{0,4},{4,0},{1,5},{5,1},{2,6},{6,2},{3,7},{7,3},{8,12},{12,8},{9,1... | collective-permute-start | bytes 1277960 | tf_op jit(solution)/shard_map/ppermute | solution.py:318

commit v4 on v3

--- a/solution.py
+++ b/solution.py
@@ -163,7 +163,9 @@
         product = dot(dense_ref[rows, :], scaled_ref[...])
         value = y_ref[rows, :].astype(F32) + DAMPING * scale_tile(columns, first, product)
         known_ref[rows, :] = scale_tile(columns, first, value).astype(BF16)
-    outs.append(start(known_ref, known_hbm, sems.at[1]))
+        if tile % 2 == 1:
+            near = pl.ds((tile - 1) * size, 2 * size)
+            outs.append(start(known_ref.at[near], known_hbm.at[near], sems.at[1 + tile]))
     found = tdot(known_ref[...], right_ref[...])
     low_ref[:cols, :] = found[:, rank:]
     both_ref[:, width : 2 * width, :] = found[:, :rank].reshape(parts, width, rank)
@@ -230,13 +232,22 @@
 ):
     tiles = 4
     size = dense_ref.shape[0] // tiles
+    copies = [
+        pltpu.make_async_copy(
+            dense_hbm.at[pl.ds(t * size, size)], dense_ref.at[pl.ds(t * size, size)], sems.at[t]
+        )
+        for t in range(tiles)
+    ]
     known_copy = start(known_hbm, known_ref, sems.at[tiles])
-    loads = load_tiles(dense_hbm, dense_ref, tiles, sems, 0)
+    copies[0].start()
+    copies[1].start()
     known_copy.wait()
-    for load in loads:
-        load.wait()
+    copies[2].start()
+    copies[3].start()
     outs = []
     for half in range(2):
+        copies[2 * half].wait()
+        copies[2 * half + 1].wait()
         rows = slice(half * 2 * size, (half + 1) * 2 * size)
         near = pl.ds(half * 2 * size, 2 * size)
         local_ref[rows, :] = (DAMPING * dot(dense_ref[rows, :], known_ref[...])).astype(BF16)

time: 65.8 us -> 64.4 us (0.979)
  Pallas kernels: 38.7 us -> 37.3 us
    pallas_call x6, Pallas kernels: 38.7 us -> 37.3 us  [call(): pl.pallas_call(kernel, out_shape=[out for out in outs], in_specs=[spec fo...]
  transfers between devices with their start and end apart: 10 -> 10, of which waited for: 2 -> 2; matrix products, arithmetic and copies ran while one was open for 0% -> 0% of each run, Pallas kernels for 45% -> 43%
where the time goes in v4:
time: 64.4 us; the launch traced here: 64.1 us
  Pallas kernels  37.3 us (58%)
  starting transfers between devices  21.5 us (33%)
  waiting for transfers between devices  4 us (6%)
  local copies, waits for them, and re-layouts  0.78 us (1%)
    pallas_call x6, Pallas kernels, call(): pl.pallas_call(kernel, out_shape=[out for out in outs], in_specs=[spec fo...  37.3 us
    ppermute x8, starting transfers between devices, partner(): return lax.ppermute(value, axis, pairs)  14 us
    ppermute x8, waiting for transfers between devices, partner(): return lax.ppermute(value, axis, pairs)  4 us
    all_to_all x1, starting transfers between devices, body(): both = lax.all_to_all(both, node, 0, 0, tiled=True)  3.93 us
    all_to_all x1, starting transfers between devices, body(): sib = lax.all_to_all(sib, ('rest', 'inner'), 0, 0, tiled=True)  3.64 us
  transfers between devices with their start and end apart: 10, of which 2 were waited for; matrix products, arithmetic and copies ran while one was open for 0% of the time, Pallas kernels for 43%

profile of v4, /device:TPU:0, one launch (start us, length us, event | category | flops | bytes accessed | tf_op | source)
XLA Modules:
  0.0 64.1 jit_solution(4648104296164529776)
XLA Ops:
  0.0 2.6 %shard_map.83 = f32[512,128]{1,0:T(8,128)S(1)} custom-call(f32[16,128]{1,0:T(8,128)} %bitcast.2, bf16[2048,512]{1,0:T(8,128)(2,1)} %y_hbm.5, bf16[2048,128]{1,0:T(8,128)(2,1)} %rl_hbm.3), custom_call_target="tpu_custom_call" | custom-call | flops 268435456 | bytes 1048576 | tf_op jit(solution)/shard_map/pallas_call | solution.py:28
  2.6 4.0 %collective-permute-start.1 = (f32[512,128]{1,0:T(8,128)S(1)}, f32[512,128]{1,0:T(8,128)S(1)}, u32[]{:S(2)}, u32[]{:S(2)}) collective-permute-start(f32[512,128]{1,0:T(8,128)S(1)} %shard_map.83), channel_id=1, source_target_pairs={{0,3},{1,2},{2,1},{3,0},{4,7},{5,6},{6,5},{7,4},{8,11},{9,10},{10,... | collective-permute-start | bytes 786440 | tf_op jit(solution)/shard_map/ppermute | solution.py:329
  6.6 0.5 collective-permute-start
  7.1 12.1 %shard_map.82 = (bf16[2048,512]{1,0:T(8,128)(2,1)}, bf16[2048,2048]{1,0:T(8,128)(2,1)}, f32[16,72,128]{2,1,0:T(8,128)S(1)}, f32[640,128]{1,0:T(8,128)S(1)}, f32[128,256]{1,0:T(8,128)S(1)}) custom-call(s32[16,12]{1,0:T(8,128)} %cols_hbm.1, f32[16,128]{1,0:T(8,128)} %bitcast.3, bf16[16,12,128,128]{3,2,1,0:T(8,128)(2,1)} %blocks_hbm.1, ...), custom_call_target="tpu_custom_call" | custom-call | flops 4294967296 | bytes 1048576 | tf_op jit(solution)/shard_map/pallas_call | solution.py:28
  19.2 0.0 collective-permute-done.1.refs_4_
  19.2 0.0 collective-permute-done.refs_3_
  19.2 1.6 %shard_map.84 = (f32[16,72,128]{2,1,0:T(8,128)}, f32[320,128]{1,0:T(8,128)S(1)}, f32[320,128]{1,0:T(8,128)S(1)}, f32[512,128]{1,0:T(8,128)}) custom-call(f32[16,72,128]{2,1,0:T(8,128)S(1)} %get-tuple-element.24.refs_0_, f32[640,128]{1,0:T(8,128)S(1)} %get-tuple-element.25.refs_1_, f32[128,256]{1,0:T(8,128)S(1)} %get-tuple-element.26.refs_2_, ...), custom_call_target="tpu_custom_call" | custom-call | flops 33554432 | bytes 1048576 | tf_op jit(solution)/shard_map/pallas_call | solution.py:28
  20.8 3.9 %all-to-all-start = ((f32[16,72,128]{2,1,0:T(8,128)}), f32[16,72,128]{2,1,0:T(8,128)S(1)}, u32[]{:S(2)}, u32[]{:S(2)}) async-start(f32[16,72,128]{2,1,0:T(8,128)} %get-tuple-element.27), calls=%async_computation | async-start | bytes 1179648 | tf_op jit(solution)/shard_map/all_to_all | solution.py:412
  24.8 1.9 %collective-permute-start.4 = (f32[320,128]{1,0:T(8,128)S(1)}, f32[320,128]{1,0:T(8,128)S(1)}, u32[]{:S(2)}, u32[]{:S(2)}) collective-permute-start(f32[320,128]{1,0:T(8,128)S(1)} %get-tuple-element.33), channel_id=1, source_target_pairs={{0,2},{1,3},{2,0},{3,1},{4,6},{5,7},{6,4},{7,5},{8,10},{9,11},{10,... | collective-permute-start | bytes 491528 | tf_op jit(solution)/shard_map/ppermute | solution.py:329
  26.7 1.5 %collective-permute-start.3 = (f32[320,128]{1,0:T(8,128)S(1)}, f32[320,128]{1,0:T(8,128)S(1)}, u32[]{:S(2)}, u32[]{:S(2)}) collective-permute-start(f32[320,128]{1,0:T(8,128)S(1)} %get-tuple-element.32), channel_id=1, source_target_pairs={{0,1},{1,0},{2,3},{3,2},{4,5},{5,4},{6,7},{7,6},{8,9},{9,8},{10,11... | collective-permute-start | bytes 491528 | tf_op jit(solution)/shard_map/ppermute | solution.py:329
  28.1 7.2 %shard_map.85.far_hbm = bf16[2048,256]{1,0:T(8,128)(2,1)} custom-call(f32[16,128]{1,0:T(8,128)} %bitcast.4, bf16[2048,2048]{1,0:T(8,128)(2,1)} %get-tuple-element.28.dense_hbm, bf16[2048,128]{1,0:T(8,128)(2,1)} %lu_hbm.5, bf16[2048,128]{1,0:T(8,128)(2,1)} %ll_hbm.5), custom_call_target="tpu_custom_call" | custom-call | flops 2147483648 | bytes 1048576 | tf_op jit(solution)/shard_map/pallas_call | solution.py:28
  35.3 0.0 all-to-all-done
  35.4 2.6 %collective-permute-start.2 = (f32[72,128]{1,0:T(8,128)S(1)}, f32[72,128]{1,0:T(8,128)S(1)}, u32[]{:S(2)}, u32[]{:S(2)}) collective-permute-start(f32[72,128]{1,0:T(8,128)S(1)} %reduce_sum.9), channel_id=1, source_target_pairs={{0,16},{16,0},{1,17},{17,1},{2,18},{18,2},{3,19},{19,3},{4,20},{20... | collective-permute-start | bytes 110600 | tf_op jit(solution)/shard_map/ppermute | solution.py:329
  38.0 0.0 collective-permute-done.3
  38.1 0.0 collective-permute-done.4
  38.1 2.2 %collective-permute-done.2 = f32[72,128]{1,0:T(8,128)S(1)} collective-permute-done((f32[72,128]{1,0:T(8,128)S(1)}, f32[72,128]{1,0:T(8,128)S(1)}, u32[]{:S(2)}, u32[]{:S(2)}) %collective-permute-start.2) | collective-permute-done | bytes 36896 | tf_op jit(solution)/shard_map/ppermute | solution.py:329
  40.3 0.8 %broadcast_in_dim.2 = f32[8,104,128]{2,1,0:T(8,128)} broadcast(f32[104,128]{1,0:T(8,128)S(1)} %pad_maximum_fusion), dimensions={1,2} | broadcast | bytes 479232 | tf_op jit(solution)/shard_map/broadcast_in_dim | solution.py:432
  41.1 3.6 %all-to-all-start.1 = ((f32[8,104,128]{2,1,0:T(8,128)}), f32[8,104,128]{2,1,0:T(8,128)S(1)}, u32[]{:S(2)}, u32[]{:S(2)}) async-start(f32[8,104,128]{2,1,0:T(8,128)} %broadcast_in_dim.2), calls=%async_computation.1 | async-start | bytes 851968 | tf_op jit(solution)/shard_map/all_to_all | solution.py:433
  44.7 1.9 %collective-permute-start.5 = (f32[320,128]{1,0:T(8,128)S(1)}, f32[320,128]{1,0:T(8,128)S(1)}, u32[]{:S(2)}, u32[]{:S(2)}) collective-permute-start(f32[320,128]{1,0:T(8,128)S(1)} %add.6), channel_id=1, source_target_pairs={{0,2},{1,3},{2,0},{3,1},{4,6},{5,7},{6,4},{7,5},{8,10},{9,11},{10,... | collective-permute-start | bytes 491528 | tf_op jit(solution)/shard_map/ppermute | solution.py:329
  46.7 1.5 %collective-permute-start.6 = (f32[320,128]{1,0:T(8,128)S(1)}, f32[320,128]{1,0:T(8,128)S(1)}, u32[]{:S(2)}, u32[]{:S(2)}) collective-permute-start(f32[320,128]{1,0:T(8,128)S(1)} %collective-permute-done.4), channel_id=1, source_target_pairs={{0,1},{1,0},{2,3},{3,2},{4,5},{5,4},{6,7},{7,6},{8,9},{9,8},{10,11... | collective-permute-start | bytes 491528 | tf_op jit(solution)/shard_map/ppermute | solution.py:329
  48.1 8.5 %shard_map.86.local_hbm = bf16[2048,512]{1,0:T(8,128)(2,1)} custom-call(bf16[2048,2048]{1,0:T(8,128)(2,1)} %get-tuple-element.28.dense_hbm, bf16[2048,512]{1,0:T(8,128)(2,1)} %get-tuple-element.36.known_hbm), custom_call_target="tpu_custom_call" | custom-call | flops 4294967296 | bytes 1048576 | tf_op jit(solution)/shard_map/pallas_call | solution.py:28
  56.7 0.0 collective-permute-done.6
  56.7 0.0 collective-permute-done.5.low_a_ref
  56.7 0.0 all-to-all-done.1.mine_ref
  56.7 0.1 collective-permute-start.7
  56.8 1.8 %collective-permute-done.7.other_ref = f32[8,104,128]{2,1,0:T(8,128)S(1)} collective-permute-done((f32[8,104,128]{2,1,0:T(8,128)S(1)}, f32[8,104,128]{2,1,0:T(8,128)S(1)}, u32[]{:S(2)}, u32[]{:S(2)}) %collective-permute-start.7) | collective-permute-done | bytes 426016 | tf_op jit(solution)/shard_map/ppermute | solution.py:329
  58.6 5.3 %shard_map.87 = f32[2048,512]{1,0:T(8,128)} custom-call(s32[1]{0:T(128)} %bitcast.core_ref, f32[16,128]{1,0:T(8,128)} %bitcast.5, bf16[2048,256]{1,0:T(8,128)(2,1)} %shard_map.85.far_hbm, bf16[2048,128]{1,0:T(8,128)(2,1)} %lu_hbm.5, bf16[2048,128]{1,0:T(8,128)(2,1)} %ll_hbm.5, f32[512,128]{1,0:T(8,128)} %get-tuple-element.30.sib_hbm, ...), custom_call_target="tpu_custom_call" | custom-call | flops 1073741824 | bytes 1048576 | tf_op jit(solution)/shard_map/pallas_call | solution.py:28
  (5 shorter events, 0.1 us)
Async XLA Ops:
  2.6 16.6 %collective-permute-start.1 = (f32[512,128]{1,0:T(8,128)S(1)}, f32[512,128]{1,0:T(8,128)S(1)}, u32[]{:S(2)}, u32[]{:S(2)}) collective-permute-start(f32[512,128]{1,0:T(8,128)S(1)} %shard_map.83), channel_id=1, source_target_pairs={{0,3},{1,2},{2,1},{3,0},{4,7},{5,6},{6,5},{7,4},{8,11},{9,10},{10,... | collective-permute-start | bytes 786440 | tf_op jit(solution)/shard_map/ppermute | solution.py:329
  6.6 12.6 %collective-permute-start = (f32[512,128]{1,0:T(8,128)S(1)}, f32[512,128]{1,0:T(8,128)S(1)}, u32[]{:S(2)}, u32[]{:S(2)}) collective-permute-start(f32[512,128]{1,0:T(8,128)S(1)} %shard_map.83), channel_id=1, source_target_pairs={{0,2},{1,3},{2,0},{3,1},{4,6},{5,7},{6,4},{7,5},{8,10},{9,11},{10,... | collective-permute-start | bytes 786440 | tf_op jit(solution)/shard_map/ppermute | solution.py:329
  20.8 14.5 %all-to-all-start = ((f32[16,72,128]{2,1,0:T(8,128)}), f32[16,72,128]{2,1,0:T(8,128)S(1)}, u32[]{:S(2)}, u32[]{:S(2)}) async-start(f32[16,72,128]{2,1,0:T(8,128)} %get-tuple-element.27), calls=%async_computation | async-start | bytes 1179648 | tf_op jit(solution)/shard_map/all_to_all | solution.py:412
  24.8 13.3 %collective-permute-start.4 = (f32[320,128]{1,0:T(8,128)S(1)}, f32[320,128]{1,0:T(8,128)S(1)}, u32[]{:S(2)}, u32[]{:S(2)}) collective-permute-start(f32[320,128]{1,0:T(8,128)S(1)} %get-tuple-element.33), channel_id=1, source_target_pairs={{0,2},{1,3},{2,0},{3,1},{4,6},{5,7},{6,4},{7,5},{8,10},{9,11},{10,... | collective-permute-start | bytes 491528 | tf_op jit(solution)/shard_map/ppermute | solution.py:329
  26.7 11.4 %collective-permute-start.3 = (f32[320,128]{1,0:T(8,128)S(1)}, f32[320,128]{1,0:T(8,128)S(1)}, u32[]{:S(2)}, u32[]{:S(2)}) collective-permute-start(f32[320,128]{1,0:T(8,128)S(1)} %get-tuple-element.32), channel_id=1, source_target_pairs={{0,1},{1,0},{2,3},{3,2},{4,5},{5,4},{6,7},{7,6},{8,9},{9,8},{10,11... | collective-permute-start | bytes 491528 | tf_op jit(solution)/shard_map/ppermute | solution.py:329
  35.4 4.9 %collective-permute-start.2 = (f32[72,128]{1,0:T(8,128)S(1)}, f32[72,128]{1,0:T(8,128)S(1)}, u32[]{:S(2)}, u32[]{:S(2)}) collective-permute-start(f32[72,128]{1,0:T(8,128)S(1)} %reduce_sum.9), channel_id=1, source_target_pairs={{0,16},{16,0},{1,17},{17,1},{2,18},{18,2},{3,19},{19,3},{4,20},{20... | collective-permute-start | bytes 110600 | tf_op jit(solution)/shard_map/ppermute | solution.py:329
  41.1 15.6 %all-to-all-start.1 = ((f32[8,104,128]{2,1,0:T(8,128)}), f32[8,104,128]{2,1,0:T(8,128)S(1)}, u32[]{:S(2)}, u32[]{:S(2)}) async-start(f32[8,104,128]{2,1,0:T(8,128)} %broadcast_in_dim.2), calls=%async_computation.1 | async-start | bytes 851968 | tf_op jit(solution)/shard_map/all_to_all | solution.py:433
  44.7 12.0 %collective-permute-start.5 = (f32[320,128]{1,0:T(8,128)S(1)}, f32[320,128]{1,0:T(8,128)S(1)}, u32[]{:S(2)}, u32[]{:S(2)}) collective-permute-start(f32[320,128]{1,0:T(8,128)S(1)} %add.6), channel_id=1, source_target_pairs={{0,2},{1,3},{2,0},{3,1},{4,6},{5,7},{6,4},{7,5},{8,10},{9,11},{10,... | collective-permute-start | bytes 491528 | tf_op jit(solution)/shard_map/ppermute | solution.py:329
  46.7 10.0 %collective-permute-start.6 = (f32[320,128]{1,0:T(8,128)S(1)}, f32[320,128]{1,0:T(8,128)S(1)}, u32[]{:S(2)}, u32[]{:S(2)}) collective-permute-start(f32[320,128]{1,0:T(8,128)S(1)} %collective-permute-done.4), channel_id=1, source_target_pairs={{0,1},{1,0},{2,3},{3,2},{4,5},{5,4},{6,7},{7,6},{8,9},{9,8},{10,11... | collective-permute-start | bytes 491528 | tf_op jit(solution)/shard_map/ppermute | solution.py:329
  56.7 1.8 %collective-permute-start.7 = (f32[8,104,128]{2,1,0:T(8,128)S(1)}, f32[8,104,128]{2,1,0:T(8,128)S(1)}, u32[]{:S(2)}, u32[]{:S(2)}) collective-permute-start(f32[8,104,128]{2,1,0:T(8,128)S(1)} %all-to-all-done.1.mine_ref), channel_id=1, source_target_pairs={{0,4},{4,0},{1,5},{5,1},{2,6},{6,2},{3,7},{7,3},{8,12},{12,8},{9,1... | collective-permute-start | bytes 1277960 | tf_op jit(solution)/shard_map/ppermute | solution.py:329

commit v5 on v4

--- a/solution.py
+++ b/solution.py
@@ -221,8 +221,15 @@
         spread_ref[rows, :] = scale_tile(square, leaf, left_ref[rows, :].astype(F32)).astype(BF16)
     for copy in copies:
         copy.wait()
-    far_ref[...] = (DAMPING * dot(dense_ref[...], spread_ref[...])).astype(BF16)
-    start(far_ref, far_hbm, sems.at[0]).wait()
+    half = dense_ref.shape[0] // 2
+    outs = []
+    for part in range(2):
+        rows = slice(part * half, (part + 1) * half)
+        far_ref[rows, :] = (DAMPING * dot(dense_ref[rows, :], spread_ref[...])).astype(BF16)
+        near = pl.ds(part * half, half)
+        outs.append(start(far_ref.at[near], far_hbm.at[near], sems.at[part]))
+    for out in outs:
+        out.wait()
 
 
 def local_kernel(
@@ -250,8 +257,11 @@
         copies[2 * half + 1].wait()
         rows = slice(half * 2 * size, (half + 1) * 2 * size)
         near = pl.ds(half * 2 * size, 2 * size)
-        local_ref[rows, :] = (DAMPING * dot(dense_ref[rows, :], known_ref[...])).astype(BF16)
-        outs.append(start(local_ref.at[near], local_hbm.at[near], sems.at[half]))
+        for tile in (2 * half, 2 * half + 1):
+            rows = slice(tile * size, (tile + 1) * size)
+            near = pl.ds(tile * size, size)
+            local_ref[rows, :] = (DAMPING * dot(dense_ref[rows, :], known_ref[...])).astype(BF16)
+            outs.append(start(local_ref.at[near], local_hbm.at[near], sems.at[tile]))
     for out in outs:
         out.wait()
 

time: 64.4 us -> 64.1 us (level)
  no operation moved by 1% of the time
where the time goes in v5:
time: 64.1 us; the launch traced here: 63.7 us
  Pallas kernels  37.2 us (58%)
  starting transfers between devices  21.4 us (33%)
  waiting for transfers between devices  3.99 us (6%)
  local copies, waits for them, and re-layouts  0.78 us (1%)
    pallas_call x6, Pallas kernels, call(): pl.pallas_call(kernel, out_shape=[out for out in outs], in_specs=[spec fo...  37.2 us
    ppermute x8, starting transfers between devices, partner(): return lax.ppermute(value, axis, pairs)  13.8 us
    ppermute x8, waiting for transfers between devices, partner(): return lax.ppermute(value, axis, pairs)  3.99 us
    all_to_all x1, starting transfers between devices, body(): both = lax.all_to_all(both, node, 0, 0, tiled=True)  3.92 us
    all_to_all x1, starting transfers between devices, body(): sib = lax.all_to_all(sib, ('rest', 'inner'), 0, 0, tiled=True)  3.64 us
  transfers between devices with their start and end apart: 10, of which 2 were waited for; matrix products, arithmetic and copies ran while one was open for 0% of the time, Pallas kernels for 43%

profile of v5, /device:TPU:0, one launch (start us, length us, event | category | flops | bytes accessed | tf_op | source)
XLA Modules:
  0.0 63.7 jit_solution(8284403477836029222)
XLA Ops:
  0.0 2.6 %shard_map.83 = f32[512,128]{1,0:T(8,128)S(1)} custom-call(f32[16,128]{1,0:T(8,128)} %bitcast.2, bf16[2048,512]{1,0:T(8,128)(2,1)} %y_hbm.5, bf16[2048,128]{1,0:T(8,128)(2,1)} %rl_hbm.3), custom_call_target="tpu_custom_call" | custom-call | flops 268435456 | bytes 1048576 | tf_op jit(solution)/shard_map/pallas_call | solution.py:28
  2.6 4.0 %collective-permute-start.1 = (f32[512,128]{1,0:T(8,128)S(1)}, f32[512,128]{1,0:T(8,128)S(1)}, u32[]{:S(2)}, u32[]{:S(2)}) collective-permute-start(f32[512,128]{1,0:T(8,128)S(1)} %shard_map.83), channel_id=1, source_target_pairs={{0,3},{1,2},{2,1},{3,0},{4,7},{5,6},{6,5},{7,4},{8,11},{9,10},{10,... | collective-permute-start | bytes 786440 | tf_op jit(solution)/shard_map/ppermute | solution.py:339
  6.6 0.5 collective-permute-start
  7.1 12.1 %shard_map.82 = (bf16[2048,512]{1,0:T(8,128)(2,1)}, bf16[2048,2048]{1,0:T(8,128)(2,1)}, f32[16,72,128]{2,1,0:T(8,128)S(1)}, f32[640,128]{1,0:T(8,128)S(1)}, f32[128,256]{1,0:T(8,128)S(1)}) custom-call(s32[16,12]{1,0:T(8,128)} %cols_hbm.1, f32[16,128]{1,0:T(8,128)} %bitcast.3, bf16[16,12,128,128]{3,2,1,0:T(8,128)(2,1)} %blocks_hbm.1, ...), custom_call_target="tpu_custom_call" | custom-call | flops 4294967296 | bytes 1048576 | tf_op jit(solution)/shard_map/pallas_call | solution.py:28
  19.2 0.0 collective-permute-done.1.refs_4_
  19.2 0.0 collective-permute-done.refs_3_
  19.2 1.6 %shard_map.84 = (f32[16,72,128]{2,1,0:T(8,128)}, f32[320,128]{1,0:T(8,128)S(1)}, f32[320,128]{1,0:T(8,128)S(1)}, f32[512,128]{1,0:T(8,128)}) custom-call(f32[16,72,128]{2,1,0:T(8,128)S(1)} %get-tuple-element.24.refs_0_, f32[640,128]{1,0:T(8,128)S(1)} %get-tuple-element.25.refs_1_, f32[128,256]{1,0:T(8,128)S(1)} %get-tuple-element.26.refs_2_, ...), custom_call_target="tpu_custom_call" | custom-call | flops 33554432 | bytes 1048576 | tf_op jit(solution)/shard_map/pallas_call | solution.py:28
  20.8 3.9 %all-to-all-start = ((f32[16,72,128]{2,1,0:T(8,128)}), f32[16,72,128]{2,1,0:T(8,128)S(1)}, u32[]{:S(2)}, u32[]{:S(2)}) async-start(f32[16,72,128]{2,1,0:T(8,128)} %get-tuple-element.27), calls=%async_computation | async-start | bytes 1179648 | tf_op jit(solution)/shard_map/all_to_all | solution.py:422
  24.7 1.9 %collective-permute-start.4 = (f32[320,128]{1,0:T(8,128)S(1)}, f32[320,128]{1,0:T(8,128)S(1)}, u32[]{:S(2)}, u32[]{:S(2)}) collective-permute-start(f32[320,128]{1,0:T(8,128)S(1)} %get-tuple-element.33), channel_id=1, source_target_pairs={{0,2},{1,3},{2,0},{3,1},{4,6},{5,7},{6,4},{7,5},{8,10},{9,11},{10,... | collective-permute-start | bytes 491528 | tf_op jit(solution)/shard_map/ppermute | solution.py:339
  26.7 1.5 %collective-permute-start.3 = (f32[320,128]{1,0:T(8,128)S(1)}, f32[320,128]{1,0:T(8,128)S(1)}, u32[]{:S(2)}, u32[]{:S(2)}) collective-permute-start(f32[320,128]{1,0:T(8,128)S(1)} %get-tuple-element.32), channel_id=1, source_target_pairs={{0,1},{1,0},{2,3},{3,2},{4,5},{5,4},{6,7},{7,6},{8,9},{9,8},{10,11... | collective-permute-start | bytes 491528 | tf_op jit(solution)/shard_map/ppermute | solution.py:339
  28.1 7.2 %shard_map.85.far_hbm = bf16[2048,256]{1,0:T(8,128)(2,1)} custom-call(f32[16,128]{1,0:T(8,128)} %bitcast.4, bf16[2048,2048]{1,0:T(8,128)(2,1)} %get-tuple-element.28.dense_hbm, bf16[2048,128]{1,0:T(8,128)(2,1)} %lu_hbm.5, bf16[2048,128]{1,0:T(8,128)(2,1)} %ll_hbm.5), custom_call_target="tpu_custom_call" | custom-call | flops 2147483648 | bytes 1048576 | tf_op jit(solution)/shard_map/pallas_call | solution.py:28
  35.3 0.0 all-to-all-done
  35.4 2.7 %collective-permute-start.2 = (f32[72,128]{1,0:T(8,128)S(1)}, f32[72,128]{1,0:T(8,128)S(1)}, u32[]{:S(2)}, u32[]{:S(2)}) collective-permute-start(f32[72,128]{1,0:T(8,128)S(1)} %reduce_sum.9), channel_id=1, source_target_pairs={{0,16},{16,0},{1,17},{17,1},{2,18},{18,2},{3,19},{19,3},{4,20},{20... | collective-permute-start | bytes 110600 | tf_op jit(solution)/shard_map/ppermute | solution.py:339
  38.0 0.0 collective-permute-done.3
  38.1 0.0 collective-permute-done.4
  38.1 2.2 %collective-permute-done.2 = f32[72,128]{1,0:T(8,128)S(1)} collective-permute-done((f32[72,128]{1,0:T(8,128)S(1)}, f32[72,128]{1,0:T(8,128)S(1)}, u32[]{:S(2)}, u32[]{:S(2)}) %collective-permute-start.2) | collective-permute-done | bytes 36896 | tf_op jit(solution)/shard_map/ppermute | solution.py:339
  40.3 0.8 %broadcast_in_dim.2 = f32[8,104,128]{2,1,0:T(8,128)} broadcast(f32[104,128]{1,0:T(8,128)S(1)} %pad_maximum_fusion), dimensions={1,2} | broadcast | bytes 479232 | tf_op jit(solution)/shard_map/broadcast_in_dim | solution.py:442
  41.1 3.6 %all-to-all-start.1 = ((f32[8,104,128]{2,1,0:T(8,128)}), f32[8,104,128]{2,1,0:T(8,128)S(1)}, u32[]{:S(2)}, u32[]{:S(2)}) async-start(f32[8,104,128]{2,1,0:T(8,128)} %broadcast_in_dim.2), calls=%async_computation.1 | async-start | bytes 851968 | tf_op jit(solution)/shard_map/all_to_all | solution.py:443
  44.7 1.7 %collective-permute-start.5 = (f32[320,128]{1,0:T(8,128)S(1)}, f32[320,128]{1,0:T(8,128)S(1)}, u32[]{:S(2)}, u32[]{:S(2)}) collective-permute-start(f32[320,128]{1,0:T(8,128)S(1)} %add.6), channel_id=1, source_target_pairs={{0,2},{1,3},{2,0},{3,1},{4,6},{5,7},{6,4},{7,5},{8,10},{9,11},{10,... | collective-permute-start | bytes 491528 | tf_op jit(solution)/shard_map/ppermute | solution.py:339
  46.5 1.5 %collective-permute-start.6 = (f32[320,128]{1,0:T(8,128)S(1)}, f32[320,128]{1,0:T(8,128)S(1)}, u32[]{:S(2)}, u32[]{:S(2)}) collective-permute-start(f32[320,128]{1,0:T(8,128)S(1)} %collective-permute-done.4), channel_id=1, source_target_pairs={{0,1},{1,0},{2,3},{3,2},{4,5},{5,4},{6,7},{7,6},{8,9},{9,8},{10,11... | collective-permute-start | bytes 491528 | tf_op jit(solution)/shard_map/ppermute | solution.py:339
  47.9 8.4 %shard_map.86.local_hbm = bf16[2048,512]{1,0:T(8,128)(2,1)} custom-call(bf16[2048,2048]{1,0:T(8,128)(2,1)} %get-tuple-element.28.dense_hbm, bf16[2048,512]{1,0:T(8,128)(2,1)} %get-tuple-element.36.known_hbm), custom_call_target="tpu_custom_call" | custom-call | flops 4294967296 | bytes 1048576 | tf_op jit(solution)/shard_map/pallas_call | solution.py:28
  56.3 0.0 collective-permute-done.6
  56.3 0.0 collective-permute-done.5.low_a_ref
  56.3 0.0 all-to-all-done.1.mine_ref
  56.4 0.1 collective-permute-start.7
  56.4 1.8 %collective-permute-done.7.other_ref = f32[8,104,128]{2,1,0:T(8,128)S(1)} collective-permute-done((f32[8,104,128]{2,1,0:T(8,128)S(1)}, f32[8,104,128]{2,1,0:T(8,128)S(1)}, u32[]{:S(2)}, u32[]{:S(2)}) %collective-permute-start.7) | collective-permute-done | bytes 426016 | tf_op jit(solution)/shard_map/ppermute | solution.py:339
  58.2 5.3 %shard_map.87 = f32[2048,512]{1,0:T(8,128)} custom-call(s32[1]{0:T(128)} %bitcast.core_ref, f32[16,128]{1,0:T(8,128)} %bitcast.5, bf16[2048,256]{1,0:T(8,128)(2,1)} %shard_map.85.far_hbm, bf16[2048,128]{1,0:T(8,128)(2,1)} %lu_hbm.5, bf16[2048,128]{1,0:T(8,128)(2,1)} %ll_hbm.5, f32[512,128]{1,0:T(8,128)} %get-tuple-element.30.sib_hbm, ...), custom_call_target="tpu_custom_call" | custom-call | flops 1073741824 | bytes 1048576 | tf_op jit(solution)/shard_map/pallas_call | solution.py:28
  (5 shorter events, 0.1 us)
Async XLA Ops:
  2.6 16.6 %collective-permute-start.1 = (f32[512,128]{1,0:T(8,128)S(1)}, f32[512,128]{1,0:T(8,128)S(1)}, u32[]{:S(2)}, u32[]{:S(2)}) collective-permute-start(f32[512,128]{1,0:T(8,128)S(1)} %shard_map.83), channel_id=1, source_target_pairs={{0,3},{1,2},{2,1},{3,0},{4,7},{5,6},{6,5},{7,4},{8,11},{9,10},{10,... | collective-permute-start | bytes 786440 | tf_op jit(solution)/shard_map/ppermute | solution.py:339
  6.6 12.6 %collective-permute-start = (f32[512,128]{1,0:T(8,128)S(1)}, f32[512,128]{1,0:T(8,128)S(1)}, u32[]{:S(2)}, u32[]{:S(2)}) collective-permute-start(f32[512,128]{1,0:T(8,128)S(1)} %shard_map.83), channel_id=1, source_target_pairs={{0,2},{1,3},{2,0},{3,1},{4,6},{5,7},{6,4},{7,5},{8,10},{9,11},{10,... | collective-permute-start | bytes 786440 | tf_op jit(solution)/shard_map/ppermute | solution.py:339
  20.8 14.5 %all-to-all-start = ((f32[16,72,128]{2,1,0:T(8,128)}), f32[16,72,128]{2,1,0:T(8,128)S(1)}, u32[]{:S(2)}, u32[]{:S(2)}) async-start(f32[16,72,128]{2,1,0:T(8,128)} %get-tuple-element.27), calls=%async_computation | async-start | bytes 1179648 | tf_op jit(solution)/shard_map/all_to_all | solution.py:422
  24.7 13.3 %collective-permute-start.4 = (f32[320,128]{1,0:T(8,128)S(1)}, f32[320,128]{1,0:T(8,128)S(1)}, u32[]{:S(2)}, u32[]{:S(2)}) collective-permute-start(f32[320,128]{1,0:T(8,128)S(1)} %get-tuple-element.33), channel_id=1, source_target_pairs={{0,2},{1,3},{2,0},{3,1},{4,6},{5,7},{6,4},{7,5},{8,10},{9,11},{10,... | collective-permute-start | bytes 491528 | tf_op jit(solution)/shard_map/ppermute | solution.py:339
  26.7 11.3 %collective-permute-start.3 = (f32[320,128]{1,0:T(8,128)S(1)}, f32[320,128]{1,0:T(8,128)S(1)}, u32[]{:S(2)}, u32[]{:S(2)}) collective-permute-start(f32[320,128]{1,0:T(8,128)S(1)} %get-tuple-element.32), channel_id=1, source_target_pairs={{0,1},{1,0},{2,3},{3,2},{4,5},{5,4},{6,7},{7,6},{8,9},{9,8},{10,11... | collective-permute-start | bytes 491528 | tf_op jit(solution)/shard_map/ppermute | solution.py:339
  35.4 4.9 %collective-permute-start.2 = (f32[72,128]{1,0:T(8,128)S(1)}, f32[72,128]{1,0:T(8,128)S(1)}, u32[]{:S(2)}, u32[]{:S(2)}) collective-permute-start(f32[72,128]{1,0:T(8,128)S(1)} %reduce_sum.9), channel_id=1, source_target_pairs={{0,16},{16,0},{1,17},{17,1},{2,18},{18,2},{3,19},{19,3},{4,20},{20... | collective-permute-start | bytes 110600 | tf_op jit(solution)/shard_map/ppermute | solution.py:339
  41.1 15.3 %all-to-all-start.1 = ((f32[8,104,128]{2,1,0:T(8,128)}), f32[8,104,128]{2,1,0:T(8,128)S(1)}, u32[]{:S(2)}, u32[]{:S(2)}) async-start(f32[8,104,128]{2,1,0:T(8,128)} %broadcast_in_dim.2), calls=%async_computation.1 | async-start | bytes 851968 | tf_op jit(solution)/shard_map/all_to_all | solution.py:443
  44.7 11.6 %collective-permute-start.5 = (f32[320,128]{1,0:T(8,128)S(1)}, f32[320,128]{1,0:T(8,128)S(1)}, u32[]{:S(2)}, u32[]{:S(2)}) collective-permute-start(f32[320,128]{1,0:T(8,128)S(1)} %add.6), channel_id=1, source_target_pairs={{0,2},{1,3},{2,0},{3,1},{4,6},{5,7},{6,4},{7,5},{8,10},{9,11},{10,... | collective-permute-start | bytes 491528 | tf_op jit(solution)/shard_map/ppermute | solution.py:339
  46.5 9.8 %collective-permute-start.6 = (f32[320,128]{1,0:T(8,128)S(1)}, f32[320,128]{1,0:T(8,128)S(1)}, u32[]{:S(2)}, u32[]{:S(2)}) collective-permute-start(f32[320,128]{1,0:T(8,128)S(1)} %collective-permute-done.4), channel_id=1, source_target_pairs={{0,1},{1,0},{2,3},{3,2},{4,5},{5,4},{6,7},{7,6},{8,9},{9,8},{10,11... | collective-permute-start | bytes 491528 | tf_op jit(solution)/shard_map/ppermute | solution.py:339
  56.4 1.8 %collective-permute-start.7 = (f32[8,104,128]{2,1,0:T(8,128)S(1)}, f32[8,104,128]{2,1,0:T(8,128)S(1)}, u32[]{:S(2)}, u32[]{:S(2)}) collective-permute-start(f32[8,104,128]{2,1,0:T(8,128)S(1)} %all-to-all-done.1.mine_ref), channel_id=1, source_target_pairs={{0,4},{4,0},{1,5},{5,1},{2,6},{6,2},{3,7},{7,3},{8,12},{12,8},{9,1... | collective-permute-start | bytes 1277960 | tf_op jit(solution)/shard_map/ppermute | solution.py:339
